TPU v7x, 32 devices: a whole 2x2x4 slice. The times are simulated.
32 devices in a mesh: span: 8 (over z, y), plane: 4 (over x, core).
Axes of the slice: x: 2, y: 2, z: 4, core: 2. Of those that a mesh axis runs over, the one named last changes fastest.
Arguments:
- adjoint: float32 [3, 32, 81, 512], P(None, 'span', None, 'plane'), may hold values from -6 to 6
- checkpoints: bfloat16 [8, 2, 32, 81, 512], P(None, None, 'span', None, 'plane'), may hold values from -4 to 4
- checkpoint_step: int32 [3], replicated, may hold values from 0 to 7
- metric: float32 [2, 512], P(None, 'plane'), may hold values from 0.004 to 0.016
- helmholtz_inverse: float32 [32, 81, 81], P('span'), may hold values from -0.08 to 0.8
- wall_element: int32 [1024, 2], replicated, may hold values from 0 to 511
- wall_local: int32 [1024, 2], replicated, may hold values from 0 to 80
- wall_weight: float32 [32, 1024], P('span'), may hold values from 0.7 to 140
Outputs:
- adjoint_next: float32 [3, 32, 81, 512], P(None, 'span', None, 'plane')
- control_gradient: float32 [32, 1024], P('span', 'plane')
All inputs are finite; a program needn't handle non-finite values.
Results may differ from a plain program's by a relative error of at most 0.00065.
Values may be sent and summed in bfloat16 or wider, within the bound.
A program may use at most 128 MiB of HBM per device.

v0:
```python
import jax
import jax.numpy as jnp
import numpy as np
from jax import lax
from jax.sharding import PartitionSpec as P

P_SIZE = 8
NSTEP = 3


HIGHEST = lax.Precision.HIGHEST


def chebyshev_matrix(degree):
    points = np.arange(degree + 1)
    abscissa = np.cos(np.pi * points / degree)
    signed = np.where((points == 0) | (points == degree), 2.0, 1.0) * (-1.0) ** points
    spacing = abscissa[:, None] - abscissa[None, :] + np.eye(degree + 1)
    matrix = signed[:, None] / signed[None, :] / spacing
    return matrix - np.eye(degree + 1) * np.sum(matrix, axis=1)[:, None]


def fourier_table(length):
    row_index = np.arange(length)[:, None]
    column = np.arange(length)[None, :]
    wavenumber = (row_index + 1) // 2
    phase_angle = 2.0 * np.pi * wavenumber * column / length
    parity = row_index % 2
    base_rows = np.where(
        row_index == 0, 1.0, np.where(parity == 1, np.cos(phase_angle), np.sin(phase_angle))
    )
    row_scale = np.where(
        (row_index == 0) | (row_index == length - 1), 1.0 / np.sqrt(length), np.sqrt(2.0 / length)
    )
    return base_rows * row_scale


def transport(field_data, velocity, metric):
    side_nodes = P_SIZE + 1
    matrix = jnp.asarray(chebyshev_matrix(P_SIZE), jnp.float32)
    shaped = field_data.reshape(
        field_data.shape[0], field_data.shape[1], side_nodes, side_nodes, field_data.shape[3]
    )
    first_dir = jnp.einsum("ai,czibe->czabe", matrix, shaped, precision=HIGHEST).reshape(
        field_data.shape
    )
    second_dir = jnp.einsum("bi,czaie->czabe", matrix, shaped, precision=HIGHEST).reshape(
        field_data.shape
    )
    speed_data = velocity.astype(jnp.float32)
    return (
        field_data
        + speed_data[0] * (metric[0] * first_dir)
        + speed_data[1] * (metric[1] * second_dir)
    )


def forward_modes(gathered):
    basis_table = jnp.asarray(fourier_table(gathered.shape[1]), jnp.float32)
    return jnp.einsum("jz,czqe->cjqe", basis_table, gathered, precision=HIGHEST)


def backward_planes(solved):
    basis_table = jnp.asarray(fourier_table(solved.shape[1]), jnp.float32)
    return jnp.einsum("jz,cjqe->czqe", basis_table, solved, precision=HIGHEST)


def solve_modes(inverse_block, coefficients):
    return jnp.einsum("jqr,cjre->cjqe", inverse_block, coefficients, precision=HIGHEST)


def to_plane_layout(point_data):
    return lax.all_to_all(point_data, "span", split_axis=1, concat_axis=3, tiled=True)


def wall_terms(field_one, speed_one, flat_index, inside, wall_count):
    rows = field_one.shape[0]
    values = jnp.take(field_one.reshape(rows, -1), flat_index, axis=1)
    speeds = jnp.take(speed_one.reshape(rows, -1), flat_index, axis=1).astype(jnp.float32)
    product = jnp.where(inside, values * speeds, 0.0).reshape(rows, wall_count, 2)
    return jnp.sum(product, axis=2)


def on_device(
    adjoint,
    checkpoints,
    checkpoint_step,
    metric,
    helmholtz_inverse,
    wall_element,
    wall_local,
    wall_weight,
):
    planes_dev = adjoint.shape[1]
    elems_dev = adjoint.shape[3]
    wall_count = wall_element.shape[0]
    span_count = lax.axis_size("span")
    all_modes = lax.all_gather(helmholtz_inverse, "span", axis=0, tiled=True)
    offset = lax.axis_index("plane") * elems_dev
    local_element = wall_element - offset
    inside = ((local_element >= 0) & (local_element < elems_dev)).reshape(-1)
    flat_index = (wall_local * elems_dev + jnp.clip(local_element, 0, elems_dev - 1)).reshape(-1)
    partial_sum = jnp.zeros((planes_dev, wall_count), jnp.float32)
    for substep in range(NSTEP):
        velocity = lax.dynamic_index_in_dim(
            checkpoints, checkpoint_step[substep], 0, keepdims=False
        )
        advected = transport(adjoint, velocity, metric)
        point_data = backward_planes(
            solve_modes(
                all_modes,
                forward_modes(
                    lax.all_to_all(advected, "span", split_axis=3, concat_axis=1, tiled=True)
                ),
            )
        )
        adjoint = to_plane_layout(point_data)
        partial_sum = partial_sum + wall_terms(
            adjoint[1], velocity[1], flat_index, inside, wall_count
        )
    weighted = wall_weight * partial_sum
    grad_share = lax.psum_scatter(weighted, "plane", scatter_dimension=1, tiled=True)
    square_total = lax.psum(jnp.sum(grad_share * grad_share), ("span", "plane"))
    inverse_rms = lax.rsqrt(square_total / (planes_dev * span_count * wall_count) + 1e-06)
    return (adjoint, grad_share * inverse_rms)


def solution(mesh):
    placed = (
        P(None, "span", None, "plane"),
        P(None, None, "span", None, "plane"),
        P(),
        P(None, "plane"),
        P("span", None, None),
        P(),
        P(),
        P("span", None),
    )
    return jax.shard_map(
        on_device,
        mesh=mesh,
        in_specs=placed,
        out_specs=(P(None, "span", None, "plane"), P("span", "plane")),
        check_vma=False,
    )
```

profile of v0, /device:TPU:0, one launch (start us, length us, event | category | flops | bytes accessed | tf_op | source)
XLA Modules:
  0.0 388.5 jit_solution(4690724075645304346)
XLA Ops:
  7.2 1.4 fusion.34
  12.6 1.9 convolution_bitcast_fusion.4
  19.3 1.2 copy.127
  20.4 7.3 %all-to-all-start = ((f32[3,4,81,128]{2,1,0,3:T(4,128)}), f32[3,4,81,128]{2,1,0,3:T(4,128)S(1)}, u32[]{:S(2)}, u32[]{:S(2)}) async-start(f32[3,4,81,128]{2,1,0,3:T(4,128)} %copy.127), calls=%async_computation | async-start | bytes 1572864 | tf_op jit(solution)/shard_map/all_to_all | solution.py:113
  27.8 47.5 %all_gather.3 = f32[32,81,81]{2,1,0:T(8,128)S(1)} all-gather(f32[4,81,81]{2,1,0:T(8,128)S(1)} %copy.131), channel_id=1, replica_groups=mesh['span'=8,'plane'=4] {'span'}, dimensions={0}, use_global_device_ids=true | all-gather | bytes 944784 | tf_op jit(solution)/shard_map/all_gather | solution.py:98
  77.0 2.7 fusion.6
  80.8 1.3 copy.135
  82.1 3.7 all-to-all-start.1
  86.6 15.1 %all-to-all-done.1 = f32[3,32,81,16]{2,3,0,1:T(8,128)S(1)} async-done(((f32[3,32,81,16]{2,3,0,1:T(8,128)}), f32[3,32,81,16]{2,3,0,1:T(8,128)S(1)}, u32[]{:S(2)}, u32[]{:S(2)}) %all-to-all-start.1) | async-done | bytes 497696 | tf_op jit(solution)/shard_map/all_to_all | solution.py:73
  101.7 3.0 copy.136
  104.7 3.2 reshape.90
  107.9 1.8 convolution_bitcast_fusion.2
  109.7 1.8 convolution_bitcast_fusion.3
  112.5 2.3 copy.140
  116.6 21.5 %all_to_all.108 = f32[3,4,81,128]{2,1,0,3:T(4,128)S(1)} all-to-all(f32[3,4,81,128]{2,1,0,3:T(4,128)S(1)} %copy.143), channel_id=1, replica_groups=mesh['span'=8,'plane'=4] {'span'}, dimensions={3} | all-to-all | bytes 995328 | tf_op jit(solution)/shard_map/all_to_all | solution.py:113
  139.9 2.7 fusion.9
  144.1 22.7 %all_to_all.109 = f32[3,32,81,16]{2,3,0,1:T(8,128)S(1)} all-to-all(f32[3,32,81,16]{2,3,0,1:T(8,128)S(1)} %copy.150), channel_id=1, replica_groups=mesh['span'=8,'plane'=4] {'span'}, dimensions={1} | all-to-all | bytes 995328 | tf_op jit(solution)/shard_map/all_to_all | solution.py:73
  166.7 3.1 copy.151
  169.8 3.2 reshape.93
  173.0 1.9 convolution_bitcast_fusion
  174.9 1.8 convolution_bitcast_fusion.1
  177.7 2.3 copy.155
  181.2 1.2 copy.158
  182.4 3.6 all-to-all-start.4
  186.0 19.8 %all-to-all-done.4 = f32[3,4,81,128]{2,1,0,3:T(4,128)S(1)} async-done(((f32[3,4,81,128]{2,1,0,3:T(4,128)}), f32[3,4,81,128]{2,1,0,3:T(4,128)S(1)}, u32[]{:S(2)}, u32[]{:S(2)}) %all-to-all-start.4) | async-done | bytes 497696 | tf_op jit(solution)/shard_map/all_to_all | solution.py:113
  207.1 2.7 fusion.12
  210.8 1.4 copy.165
  212.2 3.5 all-to-all-start.5
  218.1 2.6 copy.172
  220.8 2.3 copy.174
  223.1 7.7 %gather_fusion.3 = bf16[2048,4]{1,0:T(8,128)(2,1)S(1)} fusion(bf16[4,10368]{0,1:T(8,128)(2,1)} %bitcast.184, s32[2048]{0:T(1024)S(1)} %fusion.33), kind=kCustom, calls=%fused_computation.4.clone | custom fusion | bytes 40960 | tf_op jit(solution)/shard_map/jit(_take)/gather | solution.py:79
  230.8 9.7 %gather_fusion.5 = bf16[2048,4]{1,0:T(8,128)(2,1)} fusion(bf16[4,10368]{0,1:T(8,128)(2,1)} %bitcast.185, s32[2048]{0:T(1024)S(1)} %fusion.33), kind=kCustom, calls=%fused_computation.5.clone | custom fusion | bytes 40960 | tf_op jit(solution)/shard_map/jit(_take)/gather | solution.py:79
  240.5 2.4 copy.170
  242.9 9.8 %gather_fusion.1 = bf16[2048,4]{1,0:T(8,128)(2,1)} fusion(bf16[4,10368]{0,1:T(8,128)(2,1)} %bitcast.186, s32[2048]{0:T(1024)S(1)} %fusion.33), kind=kCustom, calls=%fused_computation.1.clone | custom fusion | bytes 40960 | tf_op jit(solution)/shard_map/jit(_take)/gather | solution.py:79
  252.7 1.4 slice.102
  254.1 5.3 %copy.169 = f32[1,4,81,8,16]{1,4,3,2,0:T(8,128)} copy(f32[1,4,81,8,16]{4,3,1,2,0:T(8,128)S(1)} %slice.102) | data formatting | bytes 331776 | tf_op jit(solution)/shard_map/slice | solution.py:119
  259.4 10.1 %gather_fusion = f32[2048,4]{1,0:T(8,128)} fusion(f32[4,10368]{0,1:T(8,128)} %bitcast.167, s32[2048]{0:T(1024)S(1)} %fusion.33), kind=kCustom, calls=%fused_computation.clone | custom fusion | bytes 73728 | tf_op jit(solution)/shard_map/jit(_take)/gather | solution.py:78
  269.4 1.4 slice.103
  270.9 5.3 %copy.171 = f32[1,4,81,8,16]{1,4,3,2,0:T(8,128)} copy(f32[1,4,81,8,16]{4,3,1,2,0:T(8,128)S(1)} %slice.103) | data formatting | bytes 331776 | tf_op jit(solution)/shard_map/slice | solution.py:119
  276.2 10.1 %gather_fusion.2 = f32[2048,4]{1,0:T(8,128)} fusion(f32[4,10368]{0,1:T(8,128)} %bitcast.168, s32[2048]{0:T(1024)S(1)} %fusion.33), kind=kCustom, calls=%fused_computation.2.clone | custom fusion | bytes 73728 | tf_op jit(solution)/shard_map/jit(_take)/gather | solution.py:78
  286.3 5.7 %copy.173 = f32[1,4,81,8,16]{1,4,3,2,0:T(8,128)} copy(f32[1,4,81,8,16]{2,4,3,1,0:T(8,128)S(1)} %slice.104) | data formatting | bytes 331776 | tf_op jit(solution)/shard_map/slice | solution.py:119
  292.1 10.1 %gather_fusion.4 = f32[2048,4]{1,0:T(8,128)} fusion(f32[4,10368]{0,1:T(8,128)} %bitcast.169, s32[2048]{0:T(1024)S(1)} %fusion.33), kind=kCustom, calls=%fused_computation.3.clone | custom fusion | bytes 73728 | tf_op jit(solution)/shard_map/jit(_take)/gather | solution.py:78
  302.1 4.6 %fusion.16 = (f32[4,2048]{0,1:T(8,128)}, f32[4,2048]{0,1:T(8,128)S(1)}, f32[4,2048]{0,1:T(8,128)S(1)}) fusion(f32[2048,4]{1,0:T(8,128)} %gather_fusion.2, bf16[2048,4]{1,0:T(8,128)(2,1)S(1)} %gather_fusion.3, pred[2048]{0:T(1024)(128)(4,1)S(1)} %compare_and_fusion.1, pred[2048]{0:T(1024)(128)(4,1)S(1)} %reshape.96, bf16[2048,4]{1,0:T(8,128)(2,1)} %gather_fusion.5, ...), kind=kLoop, calls=%fused_computation.30 | loop fusion | flops 122880 | bytes 249856 | tf_op jit(solution)/shard_map/jit(_where)/select_n | solution.py:80
  306.7 2.5 reduce_sum.37
  309.2 2.3 reduce_sum.38
  311.6 1.3 reduce_sum.36
  314.7 23.1 %reduce-scatter.4.cloned.1.call-done = f32[256,4]{1,0:T(8,128)} async-done(((f32[1024,4]{1,0:T(8,128)}), f32[256,4]{1,0:T(8,128)}) %reduce-scatter.4.cloned.1.call-update) | async-done | bytes 4112
  340.4 39.5 %psum.7 = f32[]{:T(128)} all-reduce(f32[]{:T(128)} %multiply_reduce_fusion), channel_id=1, replica_groups=mesh['span'=8,'plane'=4] {'span','plane'}, use_global_device_ids=true, to_apply=%region_5.8 | all-reduce | flops 1 | bytes 8 | tf_op jit(solution)/shard_map/psum | solution.py:123
  (104 shorter events, 24.2 us)
Async XLA Ops:
  7.2 7.4 %copy-start.13 = (f32[9,9,1,1,1]{1,0,4,3,2:T(8,128)S(1)}, f32[9,9,1,1,1]{1,0,4,3,2:T(8,128)}, u32[]{:S(2)}) copy-start(f32[9,9,1,1,1]{1,0,4,3,2:T(8,128)} %constant.58) | copy-start | bytes 976
  7.2 7.4 %copy-start = (f32[3,4,81,128]{3,1,2,0:T(4,128)S(1)}, f32[3,4,81,128]{3,1,2,0:T(4,128)}, u32[]{:S(2)}) copy-start(f32[3,4,81,128]{3,1,2,0:T(4,128)} %param.21) | copy-start | bytes 1492996
  12.6 2.8 copy-start.24
  15.4 3.6 copy-start.18
  15.4 3.6 copy-start.21
  19.3 8.5 %copy-start.14 = (f32[4,81,81]{2,0,1:T(4,128)S(1)}, f32[4,81,81]{2,0,1:T(4,128)}, u32[]{:S(2)}) copy-start(f32[4,81,81]{2,0,1:T(4,128)} %param.25) | copy-start | bytes 314932
  20.4 54.8 %all-to-all-start = ((f32[3,4,81,128]{2,1,0,3:T(4,128)}), f32[3,4,81,128]{2,1,0,3:T(4,128)S(1)}, u32[]{:S(2)}, u32[]{:S(2)}) async-start(f32[3,4,81,128]{2,1,0,3:T(4,128)} %copy.127), calls=%async_computation | async-start | bytes 1572864 | tf_op jit(solution)/shard_map/all_to_all | solution.py:113
  75.2 0.7 copy-start.10
  82.1 19.6 %all-to-all-start.1 = ((f32[3,32,81,16]{2,3,0,1:T(8,128)}), f32[3,32,81,16]{2,3,0,1:T(8,128)S(1)}, u32[]{:S(2)}, u32[]{:S(2)}) async-start(f32[3,32,81,16]{2,3,0,1:T(8,128)} %copy.135), calls=%async_computation.1 | async-start | bytes 1572864 | tf_op jit(solution)/shard_map/all_to_all | solution.py:73
  111.6 3.3 copy-start.4
  112.5 2.5 copy-start.2
  114.8 1.0 copy-start.7
  114.8 1.1 copy-start.8
  114.8 1.1 copy-start.9
  114.8 1.1 copy-start.19
  114.8 1.1 copy-start.22
  138.1 0.7 copy-start.11
  176.7 3.3 copy-start.3
  177.7 2.5 copy-start.1
  179.9 1.0 copy-start.6
  179.9 1.0 copy-start.20
  179.9 1.0 copy-start.23
  182.4 23.4 %all-to-all-start.4 = ((f32[3,4,81,128]{2,1,0,3:T(4,128)}), f32[3,4,81,128]{2,1,0,3:T(4,128)S(1)}, u32[]{:S(2)}, u32[]{:S(2)}) async-start(f32[3,4,81,128]{2,1,0,3:T(4,128)} %copy.158), calls=%async_computation.4 | async-start | bytes 1572864 | tf_op jit(solution)/shard_map/all_to_all | solution.py:113
  186.0 20.0 %copy-start.12 = (f32[32,32,1,1]{1,0,3,2:T(8,128)S(1)}, f32[32,32,1,1]{1,0,3,2:T(8,128)}, u32[]{:S(2)}) copy-start(f32[32,32,1,1]{1,0,3,2:T(8,128)} %constant.59) | copy-start | bytes 12292
  210.8 5.0 %copy-start.15 = (s32[1024,2]{0,1:T(2,128)S(1)}, s32[1024,2]{0,1:T(2,128)}, u32[]{:S(2)}) copy-start(s32[1024,2]{0,1:T(2,128)} %param.26) | copy-start | bytes 24580
  210.8 5.7 %copy-start.17 = (s32[1024,2]{0,1:T(2,128)S(1)}, s32[1024,2]{0,1:T(2,128)}, u32[]{:S(2)}) copy-start(s32[1024,2]{0,1:T(2,128)} %param.27) | copy-start | bytes 24580
  212.2 74.0 %all-to-all-start.5 = ((f32[3,32,81,16]{2,3,0,1:T(8,128)}), f32[3,32,81,16]{2,3,0,1:T(8,128)S(1)}, u32[]{:S(2)}, u32[]{:S(2)}) async-start(f32[3,32,81,16]{2,3,0,1:T(8,128)} %copy.165), calls=%async_computation.5 | async-start | bytes 1572864 | tf_op jit(solution)/shard_map/all_to_all | solution.py:73
  215.8 122.0 %reduce-scatter.4.cloned.1.call-start = ((), (), s32[]{:S(2)}) async-start(), calls=%async_computation.7 | async-start | bytes 655360
  311.6 1.3 copy-start.5
  312.9 0.7 copy-start.16
Sparse Core Ops, SparseCore 0:
  314.8 22.9 reduce-scatter.3
where the time goes:
time: 396 us; the launch traced here: 388 us
  blocking collectives  131 us (33%)
  local copies, waits for them, and re-layouts  121 us (31%)
  waiting for transfers between devices  58 us (15%)
  matrix products  24.4 us (6%)
  between operations  21.7 us (5%)
  starting transfers between devices  18.2 us (5%)
  other arithmetic  13.9 us (4%)
    all_gather x1, blocking collectives, on_device(): all_modes = lax.all_gather(helmholtz_inverse, 'span', axis=0, tiled=True)  47.5 us
    psum x1, blocking collectives, on_device(): square_total = lax.psum(jnp.sum(grad_share * grad_share), ('span', 'plane'))  39.5 us
    gather x3, local copies, waits for them, and re-layouts, wall_terms(): values = jnp.take(field_one.reshape(rows, -1), flat_index, axis=1)  30.2 us
    gather x3, local copies, waits for them, and re-layouts, wall_terms(): jnp.take(speed_one.reshape(rows, -1), flat_index, axis=1)  27.2 us
    unnamed x2, waiting for transfers between devices  23.1 us
    all_to_all x1, blocking collectives, to_plane_layout(): lax.all_to_all(point_data, 'span', split_axis=1, concat_axis=3, tiled=True)  22.7 us
    all_to_all x1, blocking collectives, on_device(): lax.all_to_all(advected, 'span', split_axis=3, concat_axis=1, tiled=True)  21.5 us
    all_to_all x2, waiting for transfers between devices, on_device(): lax.all_to_all(advected, 'span', split_axis=3, concat_axis=1, tiled=True)  19.8 us
  transfers between devices with their start and end apart: 5, of which 3 were waited for; matrix products, arithmetic and copies ran while one was open for 18% of the time, Pallas kernels for 0%

commit v1 on v0

--- a/solution.py
+++ b/solution.py
@@ -95,34 +95,32 @@
     elems_dev = adjoint.shape[3]
     wall_count = wall_element.shape[0]
     span_count = lax.axis_size("span")
+    share = elems_dev // span_count
     all_modes = lax.all_gather(helmholtz_inverse, "span", axis=0, tiled=True)
     offset = lax.axis_index("plane") * elems_dev
     local_element = wall_element - offset
     inside = ((local_element >= 0) & (local_element < elems_dev)).reshape(-1)
     flat_index = (wall_local * elems_dev + jnp.clip(local_element, 0, elems_dev - 1)).reshape(-1)
-    partial_sum = jnp.zeros((planes_dev, wall_count), jnp.float32)
+    velocity = jnp.stack([
+        lax.dynamic_index_in_dim(checkpoints, checkpoint_step[s], 0, keepdims=False)
+        for s in range(NSTEP)
+    ])
+    velocity = lax.all_to_all(velocity, "span", split_axis=4, concat_axis=2, tiled=True)
+    field = lax.all_to_all(adjoint, "span", split_axis=3, concat_axis=1, tiled=True)
+    scale = lax.dynamic_slice_in_dim(metric, lax.axis_index("span") * share, share, 1)
+    product = 0.0
     for substep in range(NSTEP):
-        velocity = lax.dynamic_index_in_dim(
-            checkpoints, checkpoint_step[substep], 0, keepdims=False
-        )
-        advected = transport(adjoint, velocity, metric)
-        point_data = backward_planes(
-            solve_modes(
-                all_modes,
-                forward_modes(
-                    lax.all_to_all(advected, "span", split_axis=3, concat_axis=1, tiled=True)
-                ),
-            )
-        )
-        adjoint = to_plane_layout(point_data)
-        partial_sum = partial_sum + wall_terms(
-            adjoint[1], velocity[1], flat_index, inside, wall_count
-        )
+        advected = transport(field, velocity[substep], scale)
+        field = backward_planes(solve_modes(all_modes, forward_modes(advected)))
+        product = product + field[1] * velocity[substep, 1].astype(jnp.float32)
+    both = to_plane_layout(jnp.concatenate([field, product[None]], axis=0))
+    gathered = jnp.take(both[3].reshape(planes_dev, -1), flat_index, axis=1)
+    partial_sum = jnp.where(inside, gathered, 0.0).reshape(planes_dev, wall_count, 2).sum(axis=2)
     weighted = wall_weight * partial_sum
     grad_share = lax.psum_scatter(weighted, "plane", scatter_dimension=1, tiled=True)
     square_total = lax.psum(jnp.sum(grad_share * grad_share), ("span", "plane"))
     inverse_rms = lax.rsqrt(square_total / (planes_dev * span_count * wall_count) + 1e-06)
-    return (adjoint, grad_share * inverse_rms)
+    return (both[:3], grad_share * inverse_rms)
 
 
 def solution(mesh):

time: 396 us -> 299 us (0.76)
  blocking collectives: 131 us -> 77.4 us
  local copies, waits for them, and re-layouts: 121 us -> 79.6 us
  matrix products: 24.4 us -> 48.8 us
  waiting for transfers between devices: 58 us -> 38.8 us
    gather x6 -> x1, local copies, waits for them, and re-layouts: 57.4 us -> 7.96 us  [on_device(): gathered = jnp.take(both[3].reshape(planes_dev, -1), flat_index, axis=1)]
    all_to_all x2 -> x0, blocking collectives: 44.2 us -> none  [the longest x1 22.7 us: to_plane_layout(): lax.all_to_all(point_data, 'span', split_axis=1, concat_axis=3, tiled=True)]
    all_to_all x2, waiting for transfers between devices: 19.8 us -> 0.01 us  [the longest x1 0.01 us: on_device(): lax.all_to_all(adjoint, 'span', split_axis=3, concat_axis=1, tiled=True)]
    slice x11 -> x12, local copies, waits for them, and re-layouts: 29 us -> 9.31 us  [the longest x2 5.72 us: on_device(): gathered = jnp.take(both[3].reshape(planes_dev, -1), flat_index, axis=1)]
    reshape x1 -> x6, local copies, waits for them, and re-layouts: 0.35 us -> 13.8 us  [the longest x3 8.34 us: transport(): jnp.einsum('ai,czibe->czabe', matrix, shaped, precision=HIGHEST)]
    all_to_all x7 -> x1, local copies, waits for them, and re-layouts: 12.7 us -> 0.1 us  [to_plane_layout(): lax.all_to_all(point_data, 'span', split_axis=1, concat_axis=3, tiled=True)]
    dot_general x3, matrix products: 4.46 us -> 17 us  [transport(): jnp.einsum('ai,czibe->czabe', matrix, shaped, precision=HIGHEST)]
    all_gather x1, blocking collectives: 47.5 us -> 38 us  [on_device(): all_modes = lax.all_gather(helmholtz_inverse, 'span', axis=0, tiled=True)]
  transfers between devices with their start and end apart: 5 -> 4, of which waited for: 3 -> 2; matrix products, arithmetic and copies ran while one was open for 18% -> 14% of each run, Pallas kernels for 0% -> 0%
where the time goes in v1:
time: 299 us; the launch traced here: 294 us
  local copies, waits for them, and re-layouts  79.6 us (27%)
  blocking collectives  77.4 us (26%)
  matrix products  48.8 us (16%)
  waiting for transfers between devices  38.8 us (13%)
  between operations  21.1 us (7%)
  starting transfers between devices  17.6 us (6%)
  other arithmetic  11 us (4%)
    psum x1, blocking collectives, on_device(): square_total = lax.psum(jnp.sum(grad_share * grad_share), ('span', 'plane'))  39.5 us
    all_gather x1, blocking collectives, on_device(): all_modes = lax.all_gather(helmholtz_inverse, 'span', axis=0, tiled=True)  38 us
    unnamed x2, waiting for transfers between devices  20.6 us
    all_to_all x1, waiting for transfers between devices, to_plane_layout(): lax.all_to_all(point_data, 'span', split_axis=1, concat_axis=3, tiled=True)  18.2 us
    dot_general x3, matrix products, transport(): jnp.einsum('ai,czibe->czabe', matrix, shaped, precision=HIGHEST)  17 us
    dot_general x3, matrix products, transport(): jnp.einsum('bi,czaie->czabe', matrix, shaped, precision=HIGHEST)  13.5 us
    reshape x2, local copies, waits for them, and re-layouts, transport(): field_data.reshape(field_data.shape[0], field_data.shape[1], side_nodes,...  12 us
    transpose x3, local copies, waits for them, and re-layouts, transport(): jnp.einsum('ai,czibe->czabe', matrix, shaped, precision=HIGHEST)  8.53 us
  transfers between devices with their start and end apart: 4, of which 2 were waited for; matrix products, arithmetic and copies ran while one was open for 14% of the time, Pallas kernels for 0%

profile of v1, /device:TPU:0, one launch (start us, length us, event | category | flops | bytes accessed | tf_op | source)
XLA Modules:
  0.0 294.3 jit_solution(10901137514128044966)
XLA Ops:
  7.2 2.2 copy.182
  9.4 7.3 %all-to-all-start = ((f32[3,4,81,128]{2,1,0,3:T(4,128)}), f32[3,4,81,128]{2,1,0,3:T(4,128)S(1)}, u32[]{:S(2)}, u32[]{:S(2)}) async-start(f32[3,4,81,128]{2,1,0,3:T(4,128)} %copy.182), calls=%async_computation | async-start | bytes 1572864 | tf_op jit(solution)/shard_map/all_to_all | solution.py:109
  16.7 1.3 fusion.76
  24.6 1.3 constant_dynamic-slice_fusion.3
  26.6 1.6 pad_maximum_fusion.1
  28.2 38.0 %all_gather.3 = f32[32,81,81]{2,1,0:T(8,128)S(1)} all-gather(f32[4,81,81]{2,1,0:T(8,128)S(1)} %copy.200), channel_id=1, replica_groups=mesh['span'=8,'plane'=4] {'span'}, dimensions={0}, use_global_device_ids=true | all-gather | bytes 944784 | tf_op jit(solution)/shard_map/all_gather | solution.py:99
  66.1 4.2 %all-to-all-start.1 = ((bf16[3,2,4,81,128]{3,2,1,0,4:T(4,128)(2,1)}), bf16[3,2,4,81,128]{3,2,1,0,4:T(4,128)(2,1)}, u32[]{:S(2)}, u32[]{:S(2)}) async-start(bf16[3,2,4,81,128]{3,2,1,0,4:T(4,128)(2,1)} %pad_maximum_fusion.1), calls=%async_computation.1 | async-start | bytes 1572864 | tf_op jit(solution)/shard_map/all_to_all | solution.py:108
  70.5 4.3 %copy.191 = f32[3,8,4,81,16]{4,2,1,3,0:T(4,128)} copy(f32[3,8,4,81,16]{3,4,1,2,0:T(8,128)S(1)} %bitcast.137) | data formatting | bytes 995328 | tf_op jit(solution)/shard_map/all_to_all | solution.py:109
  74.7 1.4 copy.184
  76.1 5.8 %copy.197 = f32[3,32,9,9,16]{1,3,4,2,0:T(8,128)} copy(f32[3,32,9,9,16]{4,1,3,2,0:T(8,128)} %bitcast.129) | data formatting | bytes 995328 | tf_op jit(solution)/shard_map/reshape | solution.py:41
  81.9 6.3 %copy.192 = f32[3,32,9,9,16]{1,2,4,3,0:T(8,128)} copy(f32[3,32,9,9,16]{4,1,3,2,0:T(8,128)} %bitcast.130) | data formatting | bytes 995328 | tf_op jit(solution)/shard_map/reshape | solution.py:41
  88.1 5.3 %convolution_bitcast_fusion = f32[3,32,9,9,16]{1,3,4,2,0:T(8,128)S(1)} fusion(f32[9,9,1,1,1]{1,0,4,3,2:T(8,128)S(1)} %copy-done.19, f32[3,32,9,9,16]{1,3,4,2,0:T(8,128)} %copy.197), kind=kOutput, calls=%fused_computation.13 | convolution fusion | flops 13436928 | bytes 995652 | tf_op jit(solution)/shard_map/bi,czaie->czabe/dot_general | solution.py:47
  94.2 1.8 copy.199
  96.0 5.3 %convolution_bitcast_fusion.1 = f32[3,32,9,9,16]{1,2,4,3,0:T(8,128)S(1)} fusion(f32[9,9,1,1,1]{1,0,4,3,2:T(8,128)S(1)} %copy-done.19, f32[3,32,9,9,16]{1,2,4,3,0:T(8,128)} %copy.192), kind=kOutput, calls=%fused_computation.14 | convolution fusion | flops 13436928 | bytes 995652 | tf_op jit(solution)/shard_map/ai,czibe->czabe/dot_general | solution.py:44
  102.0 1.8 copy.194
  103.8 1.4 copy.188
  106.1 1.2 slice_convert_fusion
  108.7 2.8 fusion.26
  111.5 1.9 convolution_bitcast_fusion.6
  113.4 2.1 copy.206
  115.5 4.1 %fusion.11 = f32[3,32,9,9,16]{1,3,4,2,0:T(8,128)S(1)} fusion(f32[9,9,1,1,1]{1,0,4,3,2:T(8,128)S(1)} %copy-done.19, f32[3,32,9,9,16]{1,4,3,2,0:T(8,128)S(1)} %bitcast.127), kind=kOutput, calls=%fused_computation.10 | convolution fusion | flops 13436928 | bytes 995652 | tf_op jit(solution)/shard_map/bi,czaie->czabe/dot_general | solution.py:47
  119.6 5.7 %fusion.8 = f32[3,32,9,9,16]{1,2,4,3,0:T(8,128)} fusion(f32[9,9,1,1,1]{1,0,4,3,2:T(8,128)S(1)} %copy-done.19, f32[3,32,9,9,16]{1,4,3,2,0:T(8,128)S(1)} %bitcast.128), kind=kOutput, calls=%fused_computation.9 | convolution fusion | flops 13436928 | bytes 995652 | tf_op jit(solution)/shard_map/ai,czibe->czabe/dot_general | solution.py:44
  126.1 1.9 copy.214
  128.0 3.9 %copy.208 = f32[3,32,9,9,16]{1,4,3,2,0:T(8,128)} copy(f32[3,32,9,9,16]{1,2,4,3,0:T(8,128)} %fusion.8) | data formatting | bytes 995328 | tf_op jit(solution)/shard_map/ai,czibe->czabe/transpose | solution.py:44
  132.0 3.3 %copy.209 = f32[3,32,81,16]{2,1,3,0:T(8,128)} copy(f32[3,32,81,16]{1,3,2,0:T(8,128)} %bitcast.134) | data formatting | bytes 995328 | tf_op jit(solution)/shard_map/reshape | solution.py:44
  135.2 2.0 fusion.73
  137.6 1.8 convolution_bitcast_fusion.5
  139.3 2.7 fusion.29
  142.0 1.9 convolution_bitcast_fusion.4
  144.0 2.1 copy.220
  146.0 4.1 %fusion.17 = f32[3,32,9,9,16]{1,3,4,2,0:T(8,128)S(1)} fusion(f32[9,9,1,1,1]{1,0,4,3,2:T(8,128)S(1)} %copy-done.19, f32[3,32,9,9,16]{1,4,3,2,0:T(8,128)S(1)} %bitcast.125), kind=kOutput, calls=%fused_computation.12 | convolution fusion | flops 13436928 | bytes 995652 | tf_op jit(solution)/shard_map/bi,czaie->czabe/dot_general | solution.py:47
  150.2 6.1 %fusion.14 = f32[3,32,9,9,16]{1,2,4,3,0:T(8,128)} fusion(f32[9,9,1,1,1]{1,0,4,3,2:T(8,128)S(1)} %copy-done.19, f32[3,32,9,9,16]{1,4,3,2,0:T(8,128)S(1)} %bitcast.126), kind=kOutput, calls=%fused_computation.11 | convolution fusion | flops 13436928 | bytes 995652 | tf_op jit(solution)/shard_map/ai,czibe->czabe/dot_general | solution.py:44
  156.3 1.5 copy.232
  158.6 1.8 copy.228
  160.3 3.9 %copy.222 = f32[3,32,9,9,16]{1,4,3,2,0:T(8,128)} copy(f32[3,32,9,9,16]{1,2,4,3,0:T(8,128)} %fusion.14) | data formatting | bytes 995328 | tf_op jit(solution)/shard_map/ai,czibe->czabe/transpose | solution.py:44
  164.3 3.3 %copy.223 = f32[3,32,81,16]{2,1,3,0:T(8,128)} copy(f32[3,32,81,16]{1,3,2,0:T(8,128)} %bitcast.136) | data formatting | bytes 995328 | tf_op jit(solution)/shard_map/reshape | solution.py:44
  167.8 2.3 convolution_bitcast_fusion.3
  170.2 2.7 fusion.32
  173.9 1.1 fusion.71
  175.1 1.6 copy.233
  176.7 5.9 %all-to-all-start.2 = ((f32[4,32,81,16]{2,3,0,1:T(8,128)}), f32[4,32,81,16]{2,3,0,1:T(8,128)S(1)}, u32[]{:S(2)}, u32[]{:S(2)}) async-start(f32[4,32,81,16]{2,3,0,1:T(8,128)} %copy.233), calls=%async_computation.2 | async-start | bytes 2097152 | tf_op jit(solution)/shard_map/all_to_all | solution.py:73
  184.1 18.2 %all-to-all-done.2 = f32[4,32,81,16]{2,3,0,1:T(8,128)S(1)} async-done(((f32[4,32,81,16]{2,3,0,1:T(8,128)}), f32[4,32,81,16]{2,3,0,1:T(8,128)S(1)}, u32[]{:S(2)}, u32[]{:S(2)}) %all-to-all-start.2) | async-done | bytes 663584 | tf_op jit(solution)/shard_map/all_to_all | solution.py:73
  202.4 5.7 %copy.237 = f32[1,4,81,8,16]{1,4,3,2,0:T(8,128)} copy(f32[1,4,81,8,16]{2,4,3,1,0:T(8,128)S(1)} %slice.124) | data formatting | bytes 331776 | tf_op jit(solution)/shard_map/slice | solution.py:117
  208.1 8.0 %gather_fusion = f32[2048,4]{1,0:T(8,128)S(1)} fusion(f32[4,10368]{0,1:T(8,128)} %bitcast.141, s32[2048]{0:T(1024)S(1)} %broadcast_clamp_fusion), kind=kCustom, calls=%fused_computation | custom fusion | bytes 73728 | tf_op jit(solution)/shard_map/jit(_take)/gather | solution.py:117
  216.1 5.8 %select_reduce_fusion = f32[4,1024]{0,1:T(8,128)S(1)} fusion(f32[4,1024,2]{0,2,1:T(2,128)S(1)} %bitcast.149, pred[1024,2]{1,0:T(8,128)(4,1)S(1)} %copy.236, pred[1024,2]{1,0:T(8,128)(4,1)S(1)} %copy.235), kind=kLoop, calls=%fused_computation.32 | loop fusion | flops 20480 | bytes 53248 | tf_op jit(solution)/shard_map/reduce_sum | solution.py:118
  223.3 20.6 %reduce-scatter.4.cloned.1.call-done = f32[256,4]{1,0:T(8,128)} async-done(((f32[1024,4]{1,0:T(8,128)}), f32[256,4]{1,0:T(8,128)}) %reduce-scatter.4.cloned.1.call-update) | async-done | bytes 4112
  245.5 1.1 copy.240
  246.5 39.5 %psum.7 = f32[]{:T(128)} all-reduce(f32[]{:T(128)} %multiply_reduce_fusion), channel_id=1, replica_groups=mesh['span'=8,'plane'=4] {'span','plane'}, use_global_device_ids=true, to_apply=%region_3.4 | all-reduce | flops 1 | bytes 8 | tf_op jit(solution)/shard_map/psum | solution.py:121
  (93 shorter events, 13.6 us)
Async XLA Ops:
  7.2 19.4 %copy-start = (f32[2,128]{1,0:T(2,128)S(1)}, f32[2,128]{1,0:T(2,128)}, u32[]{:S(2)}) copy-start(f32[2,128]{1,0:T(2,128)} %param.20) | copy-start | bytes 3076
  9.4 56.8 %all-to-all-start = ((f32[3,4,81,128]{2,1,0,3:T(4,128)}), f32[3,4,81,128]{2,1,0,3:T(4,128)S(1)}, u32[]{:S(2)}, u32[]{:S(2)}) async-start(f32[3,4,81,128]{2,1,0,3:T(4,128)} %copy.182), calls=%async_computation | async-start | bytes 1572864 | tf_op jit(solution)/shard_map/all_to_all | solution.py:109
  66.1 37.6 %all-to-all-start.1 = ((bf16[3,2,4,81,128]{3,2,1,0,4:T(4,128)(2,1)}), bf16[3,2,4,81,128]{3,2,1,0,4:T(4,128)(2,1)}, u32[]{:S(2)}, u32[]{:S(2)}) async-start(bf16[3,2,4,81,128]{3,2,1,0,4:T(4,128)(2,1)} %pad_maximum_fusion.1), calls=%async_computation.1 | async-start | bytes 1572864 | tf_op jit(solution)/shard_map/all_to_all | solution.py:108
  81.9 6.3 %copy-start.19 = (f32[9,9,1,1,1]{1,0,4,3,2:T(8,128)S(1)}, f32[9,9,1,1,1]{1,0,4,3,2:T(8,128)}, u32[]{:S(2)}) copy-start(f32[9,9,1,1,1]{1,0,4,3,2:T(8,128)} %constant.60) | copy-start | bytes 976
  103.8 3.8 %copy-start.6 = (f32[3,8,4,81,16]{3,2,1,4,0:T(4,128)S(1)}, f32[3,8,4,81,16]{3,2,1,4,0:T(4,128)}, u32[]{:S(2)}) copy-start(f32[3,8,4,81,16]{3,2,1,4,0:T(4,128)} %copy.184) | copy-start | bytes 1492996
  103.8 3.8 %copy-start.7 = (f32[3,32,81,16]{2,1,3,0:T(8,128)S(1)}, f32[3,32,81,16]{2,1,3,0:T(8,128)}, u32[]{:S(2)}) copy-start(f32[3,32,81,16]{2,1,3,0:T(8,128)} %copy.199) | copy-start | bytes 1492996
  103.8 3.8 %copy-start.16 = (f32[32,32,1,1]{1,0,3,2:T(8,128)S(1)}, f32[32,32,1,1]{1,0,3,2:T(8,128)}, u32[]{:S(2)}) copy-start(f32[32,32,1,1]{1,0,3,2:T(8,128)} %constant.61) | copy-start | bytes 12292
  103.8 3.8 %copy-start.8 = (f32[3,32,81,16]{2,1,3,0:T(8,128)S(1)}, f32[3,32,81,16]{2,1,3,0:T(8,128)}, u32[]{:S(2)}) copy-start(f32[3,32,81,16]{2,1,3,0:T(8,128)} %copy.194) | copy-start | bytes 1492996
  105.2 0.9 copy-start.4
  128.0 7.2 %copy-start.12 = (f32[1,2,8,4,81,16]{4,5,2,3,1,0:T(8,128)S(1)}, f32[1,2,8,4,81,16]{4,5,2,3,1,0:T(8,128)}, u32[]{:S(2)}) copy-start(f32[1,2,8,4,81,16]{4,5,2,3,1,0:T(8,128)} %get-tuple-element.15) | copy-start | bytes 995332
  132.0 5.6 %copy-start.2 = (f32[3,32,81,16]{2,1,3,0:T(8,128)S(1)}, f32[3,32,81,16]{2,1,3,0:T(8,128)}, u32[]{:S(2)}) copy-start(f32[3,32,81,16]{2,1,3,0:T(8,128)} %convolution_bitcast_fusion.6) | copy-start | bytes 1492996
  132.0 5.6 %copy-start.9 = (f32[3,32,81,16]{2,1,3,0:T(8,128)S(1)}, f32[3,32,81,16]{2,1,3,0:T(8,128)}, u32[]{:S(2)}) copy-start(f32[3,32,81,16]{2,1,3,0:T(8,128)} %copy.214) | copy-start | bytes 1492996
  135.2 2.3 copy-start.10
  137.4 4.6 %copy-start.17 = (f32[32,32,1,1]{1,0,3,2:T(8,128)S(1)}, f32[32,32,1,1]{1,0,3,2:T(8,128)}, u32[]{:S(2)}) copy-start(f32[32,32,1,1]{1,0,3,2:T(8,128)} %constant.61) | copy-start | bytes 12292
  150.2 6.1 %copy-start.5 = (bf16[3,2,4,81,128]{3,4,2,1,0:T(8,128)(2,1)S(1)}, bf16[3,2,4,81,128]{3,4,2,1,0:T(8,128)(2,1)}, u32[]{:S(2)}) copy-start(bf16[3,2,4,81,128]{3,4,2,1,0:T(8,128)(2,1)} %copy-done.4) | copy-start | bytes 1492996
  160.3 7.2 %copy-start.15 = (f32[1,1,8,4,81,16]{4,5,2,3,1,0:T(8,128)S(1)}, f32[1,1,8,4,81,16]{4,5,2,3,1,0:T(8,128)}, u32[]{:S(2)}) copy-start(f32[1,1,8,4,81,16]{4,5,2,3,1,0:T(8,128)} %get-tuple-element.19) | copy-start | bytes 497668
  160.3 7.3 %copy-start.14 = (f32[1,1,8,4,81,16]{4,5,2,3,1,0:T(8,128)S(1)}, f32[1,1,8,4,81,16]{4,5,2,3,1,0:T(8,128)}, u32[]{:S(2)}) copy-start(f32[1,1,8,4,81,16]{4,5,2,3,1,0:T(8,128)} %get-tuple-element.18) | copy-start | bytes 497668
  164.3 3.5 %copy-start.3 = (f32[3,32,81,16]{2,1,3,0:T(8,128)S(1)}, f32[3,32,81,16]{2,1,3,0:T(8,128)}, u32[]{:S(2)}) copy-start(f32[3,32,81,16]{2,1,3,0:T(8,128)} %convolution_bitcast_fusion.4) | copy-start | bytes 1492996
  164.3 3.6 %copy-start.11 = (f32[3,32,81,16]{2,1,3,0:T(8,128)S(1)}, f32[3,32,81,16]{2,1,3,0:T(8,128)}, u32[]{:S(2)}) copy-start(f32[3,32,81,16]{2,1,3,0:T(8,128)} %copy.228) | copy-start | bytes 1492996
  167.7 5.1 %copy-start.18 = (f32[32,32,1,1]{1,0,3,2:T(8,128)S(1)}, f32[32,32,1,1]{1,0,3,2:T(8,128)}, u32[]{:S(2)}) copy-start(f32[32,32,1,1]{1,0,3,2:T(8,128)} %constant.61) | copy-start | bytes 12292
  167.8 6.1 %copy-start.13 = (bf16[3,2,8,4,81,16]{4,3,2,5,1,0:T(4,128)(2,1)S(1)}, bf16[3,2,8,4,81,16]{4,3,2,5,1,0:T(4,128)(2,1)}, u32[]{:S(2)}) copy-start(bf16[3,2,8,4,81,16]{4,3,2,5,1,0:T(4,128)(2,1)} %copy.232) | copy-start | bytes 1492996
  173.9 8.9 %copy-start.21 = (s32[1024,2]{0,1:T(2,128)S(1)}, s32[1024,2]{0,1:T(2,128)}, u32[]{:S(2)}) copy-start(s32[1024,2]{0,1:T(2,128)} %param.22) | copy-start | bytes 24580
  173.9 8.9 %copy-start.22 = (s32[1024,2]{0,1:T(2,128)S(1)}, s32[1024,2]{0,1:T(2,128)}, u32[]{:S(2)}) copy-start(s32[1024,2]{0,1:T(2,128)} %param.23) | copy-start | bytes 24580
  176.7 25.5 %all-to-all-start.2 = ((f32[4,32,81,16]{2,3,0,1:T(8,128)}), f32[4,32,81,16]{2,3,0,1:T(8,128)S(1)}, u32[]{:S(2)}, u32[]{:S(2)}) async-start(f32[4,32,81,16]{2,3,0,1:T(8,128)} %copy.233), calls=%async_computation.2 | async-start | bytes 2097152 | tf_op jit(solution)/shard_map/all_to_all | solution.py:73
  182.6 61.2 %reduce-scatter.4.cloned.1.call-start = ((), (), s32[]{:S(2)}) async-start(), calls=%async_computation.4 | async-start | bytes 655360
  202.4 19.7 %copy-start.20 = (f32[4,1024]{1,0:T(4,128)S(1)}, f32[4,1024]{1,0:T(4,128)}, u32[]{:S(2)}) copy-start(f32[4,1024]{1,0:T(4,128)} %param.24) | copy-start | bytes 49156
  202.4 84.9 %copy-start.1 = (f32[2,128]{1,0:T(2,128)S(1)}, f32[2,128]{1,0:T(2,128)}, u32[]{:S(2)}) copy-start(f32[2,128]{1,0:T(2,128)} %param.20) | copy-start | bytes 3076
Sparse Core Ops, SparseCore 0:
  223.3 20.4 reduce-scatter.3

commit v2 on v1

--- a/solution.py
+++ b/solution.py
@@ -1,7 +1,12 @@
+import functools
+
 import jax
 import jax.numpy as jnp
+import ml_dtypes
 import numpy as np
 from jax import lax
+from jax.experimental import pallas as pl
+from jax.experimental.pallas import tpu as pltpu
 from jax.sharding import PartitionSpec as P
 
 P_SIZE = 8
@@ -123,6 +128,457 @@
     return (both[:3], grad_share * inverse_rms)
 
 
+MESH = pl.DeviceIdType.MESH
+F32 = jnp.float32
+BF16 = jnp.bfloat16
+LANES = 128
+
+
+def swap_blocks(parts, share):
+    count = len(parts)
+    width = count * share
+    lane = lax.broadcasted_iota(jnp.int32, parts[0].shape, 1)
+    k = count // 2
+    while k:
+        upper = (lane // (k * share)) % 2 == 1
+        new = list(parts)
+        for i in range(count):
+            if (i // k) % 2 == 0:
+                a, b = parts[i], parts[i + k]
+                new[i] = jnp.where(upper, pltpu.roll(b, k * share, 1), a)
+                new[i + k] = jnp.where(upper, b, pltpu.roll(a, width - k * share, 1))
+        parts = new
+        k //= 2
+    return parts
+
+
+def greet(spans, planes):
+    me, p = lax.axis_index("span"), lax.axis_index("plane")
+    barrier = pltpu.get_barrier_semaphore()
+    for o in range(1, spans):
+        pl.semaphore_signal(barrier, 1, device_id={"span": (me + o) % spans}, device_id_type=MESH)
+    for o in range(1, planes):
+        pl.semaphore_signal(barrier, 1, device_id={"plane": (p + o) % planes}, device_id_type=MESH)
+    pl.semaphore_wait(barrier, spans + planes - 2)
+
+
+def remote(src, dst, sems, kind, o, target):
+    return pltpu.make_async_remote_copy(
+        src_ref=src, dst_ref=dst, send_sem=sems.at[0, kind, o], recv_sem=sems.at[1, kind, o],
+        device_id=target, device_id_type=MESH,
+    )
+
+
+def enter_kernel(spans, planes, zdev, q, qp,
+                 step_ref, adj_ref, ck_ref, inv_ref,
+                 xs_ref, vs_ref, modes_ref,
+                 tail, snd, rcv, vsnd, vrcv, sems, local_sem):
+    share = LANES // spans
+    me, p = lax.axis_index("span"), lax.axis_index("plane")
+    bulk = q - 1
+    half = bulk // 2
+    slabs = 3 * zdev
+    sets = 2 * slabs // spans
+    greet(spans, planes)
+
+    def span_to(o):
+        return {"span": (me + o) % spans}
+
+    xpeer = {"plane": (p + 2) % planes}
+    cpeer = {"plane": p + 1 - 2 * (p % 2)}
+    px = (p + 2) % planes
+    pc = p + 1 - 2 * (p % 2)
+    pcx = (pc + 2) % planes
+    stage1, stage2x, stage2c, stage3 = [], [], [], []
+    for o in range(1, spans):
+        s = (me + spans - o) % spans
+        out = remote(inv_ref.at[p], modes_ref.at[p, me], sems, 0, o, span_to(o))
+        out.start()
+        stage1.append((out, remote(inv_ref.at[p], modes_ref.at[p, s], sems, 0, o, span_to(o))))
+        stage2x.append((remote(modes_ref.at[p, s], modes_ref.at[p, s], sems, 1, o, xpeer),
+                        remote(modes_ref.at[p, s], modes_ref.at[px, s], sems, 1, o, xpeer)))
+        stage2c.append((remote(modes_ref.at[p, s], modes_ref.at[p, s], sems, 2, o, cpeer),
+                        remote(modes_ref.at[p, s], modes_ref.at[pc, s], sems, 2, o, cpeer)))
+        stage3.append((remote(modes_ref.at[px, s], modes_ref.at[px, s], sems, 3, o, cpeer),
+                       remote(modes_ref.at[px, s], modes_ref.at[pcx, s], sems, 3, o, cpeer)))
+
+    tail[...] = jnp.zeros_like(tail)
+    for k in range(slabs):
+        tail[k % spans, k // spans:k // spans + 1, :] = adj_ref[k // zdev, k % zdev, bulk:q, :]
+    for t in range(NSTEP):
+        slot = step_ref[t]
+        for k in range(2 * zdev):
+            row = ck_ref[slot, k // zdev, k % zdev].astype(F32)[bulk:q, :]
+            tail[k, 2 + t:3 + t, :] = row
+    for i in range(sets):
+        parts = []
+        for g in range(spans):
+            h = spans * i + g
+            k, r = h // 2, (h % 2) * half
+            parts.append(adj_ref[k // zdev, k % zdev, r:r + half, :])
+        parts = swap_blocks(parts, share)
+        for d in range(spans):
+            snd[d, i * half:(i + 1) * half, :] = parts[d]
+    parts = swap_blocks([tail[g] for g in range(spans)], share)
+    for d in range(spans):
+        snd[d, sets * half:, :] = parts[d]
+    fields, speeds = [], []
+    for o in range(1, spans):
+        to, s = (me + o) % spans, (me + spans - o) % spans
+        out = remote(snd.at[to], rcv.at[me], sems, 4, o, span_to(o))
+        out.start()
+        fields.append((out, remote(snd.at[to], rcv.at[s], sems, 4, o, span_to(o))))
+    own = pltpu.make_async_copy(snd.at[me], rcv.at[me], local_sem.at[0])
+    own.start()
+    for t in range(NSTEP):
+        slot = step_ref[t]
+        parts = [ck_ref[slot, k // zdev, k % zdev].astype(F32)[:bulk] for k in range(2 * zdev)]
+        parts = swap_blocks(parts, share)
+        for d in range(spans):
+            vsnd[d, t] = parts[d].astype(BF16)
+    for o in range(1, spans):
+        to, s = (me + o) % spans, (me + spans - o) % spans
+        out = remote(vsnd.at[to], vrcv.at[me], sems, 5, o, span_to(o))
+        out.start()
+        speeds.append((out, remote(vsnd.at[to], vrcv.at[s], sems, 5, o, span_to(o))))
+    vown = pltpu.make_async_copy(vsnd.at[me], vrcv.at[me], local_sem.at[1])
+    vown.start()
+    mine = [pltpu.make_async_copy(inv_ref.at[j], modes_ref.at[j, me], local_sem.at[2 + j])
+            for j in range(zdev)]
+    for c in mine:
+        c.start()
+    xs_ref[bulk:, :] = jnp.zeros_like(xs_ref[bulk:, :])
+    vs_ref[:, :, bulk:, :] = jnp.zeros_like(vs_ref[:, :, bulk:, :])
+
+    for o in range(spans - 1):
+        stage1[o][1].wait_recv()
+        stage2x[o][0].start()
+        stage2c[o][0].start()
+    for o in range(spans - 1):
+        stage2x[o][1].wait_recv()
+        stage3[o][0].start()
+    own.wait()
+    for c in fields:
+        c[1].wait_recv()
+    for i in range(sets):
+        parts = swap_blocks([rcv[s, i * half:(i + 1) * half, :] for s in range(spans)], share)
+        for g in range(spans):
+            h = spans * i + g
+            k, r = h // 2, (h % 2) * half
+            xs_ref[r:r + half, k * LANES:(k + 1) * LANES] = parts[g]
+    parts = swap_blocks([rcv[s, sets * half:, :] for s in range(spans)], share)
+    for k in range(slabs):
+        xs_ref[bulk:q, k * LANES:(k + 1) * LANES] = parts[k % spans][k // spans:k // spans + 1]
+    for t in range(NSTEP):
+        for k in range(2 * zdev):
+            z = k % zdev
+            vs_ref[t, k // zdev, bulk:q, z * LANES:(z + 1) * LANES] = parts[k][2 + t:3 + t]
+    vown.wait()
+    for c in speeds:
+        c[1].wait_recv()
+    for t in range(NSTEP):
+        parts = swap_blocks([vrcv[s, t].astype(F32) for s in range(spans)], share)
+        for k in range(2 * zdev):
+            z = k % zdev
+            vs_ref[t, k // zdev, :bulk, z * LANES:(z + 1) * LANES] = parts[k]
+    for c in mine:
+        c.wait()
+    for group in (stage2c, stage3):
+        for c in group:
+            c[1].wait_recv()
+    for group in (stage1, stage2x, stage2c, stage3, fields, speeds):
+        for c in group:
+            c[0].wait_send()
+
+
+def split(x):
+    high = x.astype(BF16)
+    return high, (x - high.astype(F32)).astype(BF16)
+
+
+def mul3(a, b, dims=((1,), (0,))):
+    def one(x, y):
+        return lax.dot_general(x, y, (dims, ((), ())), preferred_element_type=F32)
+    return one(a[0], b[0]) + (one(a[0], b[1]) + one(a[1], b[0]))
+
+
+def steps_kernel(spans, planes, zdev, qp,
+                 xs_ref, vs_ref, modes_ref, metric_ref, elem_ref, local_ref,
+                 basis_ref, diff_ref, place_ref,
+                 out_ref, wall_ref,
+                 field, coef, solved, product, modes_hi, modes_lo):
+    share = LANES // spans
+    wide = zdev * LANES
+    me, p = lax.axis_index("span"), lax.axis_index("plane")
+    lane = lax.broadcasted_iota(jnp.int32, (1, LANES), 1)
+    rolled = pltpu.roll(metric_ref[...], (LANES - me * share) % LANES, 1)
+    scale = jnp.where(lane < share, rolled, 0.0)
+    k = share
+    while k < LANES:
+        scale = scale + pltpu.roll(scale, k, 1)
+        k *= 2
+    for j in range(zdev):
+        for s in range(spans):
+            high, low = split(modes_ref[j, s])
+            modes_hi[j, s * qp:(s + 1) * qp, :] = high
+            modes_lo[j, s * qp:(s + 1) * qp, :] = low
+    field[...] = xs_ref[...]
+    product[...] = jnp.zeros_like(product)
+    block = lax.broadcasted_iota(jnp.int32, (1, 3 * LANES), 1) % LANES // share
+    first = jnp.concatenate([scale[0:1]] * zdev, axis=1)
+    second = jnp.concatenate([scale[1:2]] * zdev, axis=1)
+
+    def one_step(t, carry):
+        v0 = vs_ref[t, 0] * first
+        v1 = vs_ref[t, 1] * second
+        for c in range(3):
+            x = field[:, c * wide:(c + 1) * wide]
+            d = mul3((diff_ref[0], diff_ref[1]), split(x))
+            coef[c * qp:(c + 1) * qp, :] = x + v0 * d[:qp] + v1 * d[qp:]
+        y = mul3(split(coef[...]), (basis_ref[0], basis_ref[1]))
+        coef[...] = y
+        for j in range(zdev):
+            lanes = slice(j * LANES, (j + 1) * LANES)
+            x = jnp.concatenate([coef[c * qp:(c + 1) * qp, lanes] for c in range(3)], axis=1)
+            r = mul3((modes_hi[j, :, :qp], modes_lo[j, :, :qp]), split(x))
+            total = r[:qp]
+            for s in range(1, spans):
+                total = jnp.where(block == s, r[s * qp:(s + 1) * qp], total)
+            for c in range(3):
+                solved[c * qp:(c + 1) * qp, lanes] = total[:, c * LANES:(c + 1) * LANES]
+        y = mul3(split(solved[...]), (basis_ref[0], basis_ref[1]), ((1,), (1,)))
+        for c in range(3):
+            field[:, c * wide:(c + 1) * wide] = y[c * qp:(c + 1) * qp]
+        product[...] += y[qp:2 * qp] * vs_ref[t, 1]
+        return carry
+
+    lax.fori_loop(0, NSTEP, one_step, 0)
+    out_ref[...] = field[...]
+
+    high, low = split(product[...])
+    base = p * LANES + me * share
+    mode = lax.broadcasted_iota(jnp.int32, (1, qp), 1)
+    near = lane % share
+
+    def picked(row):
+        total = 0.0
+        for k in range(2):
+            pick = jnp.where(local_ref[pl.ds(row, LANES), k:k + 1] == mode, 1.0, 0.0).astype(BF16)
+            keep = elem_ref[pl.ds(row, LANES), k:k + 1] - base == near
+            keep = jnp.concatenate([jnp.where(keep, 1.0, 0.0)] * zdev, axis=1)
+            got = jnp.dot(pick, high, preferred_element_type=F32)
+            got = got + jnp.dot(pick, low, preferred_element_type=F32)
+            total = total + got * keep
+        return split(total)
+
+    for part in range(planes):
+        total = 0.0
+        for h in range(2):
+            pair = picked((part * 2 + h) * LANES)
+            for v in pair:
+                total = total + lax.dot_general(
+                    place_ref[h], v, (((1,), (1,)), ((), ())), preferred_element_type=F32)
+        for s in range(spans):
+            wall_ref[s, part] = total[s * 8:(s + 1) * 8]
+
+
+def leave_kernel(spans, planes, zdev, q, count,
+                 xs_ref, wall_ref, weight_ref,
+                 out_ref, grad_ref,
+                 tail, snd, rcv, wrcv, part, prcv, square, srcv, total, trcv, sems, local_sem):
+    share = LANES // spans
+    me, p = lax.axis_index("span"), lax.axis_index("plane")
+    bulk = q - 1
+    half = bulk // 2
+    slabs = 3 * zdev
+    sets = 2 * slabs // spans
+    greet(spans, planes)
+
+    def exchange(kind, size, axis, pick_src, dst):
+        at = lax.axis_index(axis)
+        pairs = []
+        for o in range(1, size):
+            to, s = (at + o) % size, (at + size - o) % size
+            out = remote(pick_src(to), dst.at[at], sems, kind, o, {axis: to})
+            out.start()
+            pairs.append((out, remote(pick_src(to), dst.at[s], sems, kind, o, {axis: to})))
+        return pairs
+
+    walls = exchange(0, spans, "span", lambda to: wall_ref.at[to], wrcv)
+    wown = pltpu.make_async_copy(wall_ref.at[me], wrcv.at[me], local_sem.at[0])
+    wown.start()
+    tail[...] = jnp.zeros_like(tail)
+    for k in range(slabs):
+        tail[k % spans, k // spans:k // spans + 1, :] = xs_ref[bulk:q, k * LANES:(k + 1) * LANES]
+    for i in range(sets):
+        parts = []
+        for g in range(spans):
+            h = spans * i + g
+            k, r = h // 2, (h % 2) * half
+            parts.append(xs_ref[r:r + half, k * LANES:(k + 1) * LANES])
+        parts = swap_blocks(parts, share)
+        for d in range(spans):
+            snd[d, i * half:(i + 1) * half, :] = parts[d]
+    parts = swap_blocks([tail[g] for g in range(spans)], share)
+    for d in range(spans):
+        snd[d, sets * half:, :] = parts[d]
+    fields = exchange(1, spans, "span", lambda to: snd.at[to], rcv)
+    own = pltpu.make_async_copy(snd.at[me], rcv.at[me], local_sem.at[1])
+    own.start()
+
+    wown.wait()
+    for c in walls:
+        c[1].wait_recv()
+    part[...] = sum(wrcv[s] for s in range(spans))
+    rows = exchange(2, planes, "plane", lambda to: part.at[to], prcv)
+    pown = pltpu.make_async_copy(part.at[p], prcv.at[p], local_sem.at[2])
+    pown.start()
+    pown.wait()
+    for c in rows:
+        c[1].wait_recv()
+    block = sum(prcv[s] for s in range(planes))
+    sums = jnp.concatenate([block[:zdev], block[zdev:]], axis=1)
+    weight = weight_ref[:, pl.ds(pl.multiple_of(p * 2 * LANES, 2 * LANES), 2 * LANES)]
+    weighted = weight * sums
+    sq = weighted * weighted
+    square[...] = jnp.broadcast_to(jnp.sum(sq[:, :LANES] + sq[:, LANES:], axis=0, keepdims=True), (8, LANES))
+    squares = exchange(3, spans, "span", lambda to: square, srcv)
+    srcv[me] = square[...]
+    for c in squares:
+        c[1].wait_recv()
+    total[...] = sum(srcv[s] for s in range(spans))
+    totals = exchange(4, planes, "plane", lambda to: total, trcv)
+    trcv[p] = total[...]
+    for c in totals:
+        c[1].wait_recv()
+    full = jnp.sum(sum(trcv[s] for s in range(planes))[0:1], axis=1, keepdims=True)
+    grad_ref[...] = weighted * lax.rsqrt(full / count + 1e-06)
+
+    own.wait()
+    for c in fields:
+        c[1].wait_recv()
+    for i in range(sets):
+        parts = swap_blocks([rcv[s, i * half:(i + 1) * half, :] for s in range(spans)], share)
+        for g in range(spans):
+            h = spans * i + g
+            k, r = h // 2, (h % 2) * half
+            out_ref[k // zdev, k % zdev, r:r + half, :] = parts[g]
+    parts = swap_blocks([rcv[s, sets * half:, :] for s in range(spans)], share)
+    for k in range(slabs):
+        out_ref[k // zdev, k % zdev, bulk:q, :] = parts[k % spans][k // spans:k // spans + 1]
+    for group in (walls, fields, rows, squares, totals):
+        for c in group:
+            c[0].wait_send()
+
+
+def halves(table):
+    high = table.astype(np.float32).astype(ml_dtypes.bfloat16)
+    low = (table - high.astype(np.float64)).astype(np.float32).astype(ml_dtypes.bfloat16)
+    return np.stack([high, low])
+
+
+def tables(spans, zdev, q, qp):
+    share = LANES // spans
+    fourier = fourier_table(spans * zdev)
+    order = np.array([s * zdev + z for z in range(zdev) for s in range(spans)])
+    basis = np.kron(fourier[order][:, order].T, np.eye(share))
+    side = P_SIZE + 1
+    matrix = chebyshev_matrix(P_SIZE)
+    diff = np.zeros((2 * qp, qp))
+    diff[:q, :q] = np.kron(matrix, np.eye(side))
+    diff[qp:qp + q, :q] = np.kron(np.eye(side), matrix)
+    place = np.zeros((2, spans * 8, zdev * LANES), ml_dtypes.bfloat16)
+    for h in range(2):
+        for s in range(spans):
+            for z in range(zdev):
+                at = z * LANES + s * share
+                place[h, s * 8 + h * zdev + z, at:at + share] = 1.0
+    return halves(basis), halves(diff), place
+
+
+def vmem(n):
+    return [pl.BlockSpec(memory_space=pltpu.VMEM)] * n
+
+
+def kernels_on_device(spans, planes, adjoint, checkpoints, checkpoint_step, metric,
+                      helmholtz_inverse, wall_element, wall_local, wall_weight):
+    _, zdev, q, _ = adjoint.shape
+    wall_count = wall_element.shape[0]
+    qp = -(-q // 16) * 16
+    bulk, wide = q - 1, zdev * LANES
+    rows = 3 * zdev * bulk // spans + 8
+    inverse = jnp.pad(helmholtz_inverse, ((0, 0), (0, qp - q), (0, LANES - q)))
+    shape = jax.ShapeDtypeStruct
+    field, speed, modes = pl.pallas_call(
+        functools.partial(enter_kernel, spans, planes, zdev, q, qp),
+        out_shape=(shape((qp, 3 * wide), F32), shape((NSTEP, 2, qp, wide), F32),
+                   shape((zdev, spans, qp, LANES), F32)),
+        in_specs=[pl.BlockSpec(memory_space=pltpu.SMEM)] + vmem(3),
+        out_specs=tuple(vmem(3)),
+        scratch_shapes=[
+            pltpu.VMEM((spans, 8, LANES), F32),
+            pltpu.VMEM((spans, rows, LANES), F32),
+            pltpu.VMEM((spans, rows, LANES), F32),
+            pltpu.VMEM((spans, NSTEP, bulk, LANES), BF16),
+            pltpu.VMEM((spans, NSTEP, bulk, LANES), BF16),
+            pltpu.SemaphoreType.DMA((2, 6, spans)),
+            pltpu.SemaphoreType.DMA((2 + zdev,)),
+        ],
+        compiler_params=pltpu.CompilerParams(collective_id=0, has_side_effects=True),
+        name="enter",
+    )(checkpoint_step, adjoint, checkpoints, inverse)
+    basis, diff, place = tables(spans, zdev, q, qp)
+    field, walls = pl.pallas_call(
+        functools.partial(steps_kernel, spans, planes, zdev, qp),
+        out_shape=(shape((qp, 3 * wide), F32), shape((spans, planes, 8, LANES), F32)),
+        in_specs=vmem(9),
+        out_specs=tuple(vmem(2)),
+        scratch_shapes=[
+            pltpu.VMEM((qp, 3 * wide), F32),
+            pltpu.VMEM((3 * qp, wide), F32),
+            pltpu.VMEM((3 * qp, wide), F32),
+            pltpu.VMEM((qp, wide), F32),
+            pltpu.VMEM((zdev, spans * qp, LANES), BF16),
+            pltpu.VMEM((zdev, spans * qp, LANES), BF16),
+        ],
+        name="steps",
+    )(field, speed, modes, metric, wall_element, wall_local, basis, diff, place)
+    return pl.pallas_call(
+        functools.partial(leave_kernel, spans, planes, zdev, q, float(spans * zdev * wall_count)),
+        out_shape=(shape(adjoint.shape, F32), shape((zdev, wall_count // planes), F32)),
+        in_specs=vmem(3),
+        out_specs=tuple(vmem(2)),
+        scratch_shapes=[
+            pltpu.VMEM((spans, 8, LANES), F32),
+            pltpu.VMEM((spans, rows, LANES), F32),
+            pltpu.VMEM((spans, rows, LANES), F32),
+            pltpu.VMEM((spans, planes, 8, LANES), F32),
+            pltpu.VMEM((planes, 8, LANES), F32),
+            pltpu.VMEM((planes, 8, LANES), F32),
+            pltpu.VMEM((8, LANES), F32),
+            pltpu.VMEM((spans, 8, LANES), F32),
+            pltpu.VMEM((8, LANES), F32),
+            pltpu.VMEM((planes, 8, LANES), F32),
+            pltpu.SemaphoreType.DMA((2, 5, spans)),
+            pltpu.SemaphoreType.DMA((3,)),
+        ],
+        compiler_params=pltpu.CompilerParams(collective_id=1, has_side_effects=True),
+        name="leave",
+    )(field, walls, wall_weight)
+
+
+def chosen(spans, planes, *args):
+    zdev, q, elems = args[0].shape[1:]
+    walls = args[5].shape[0]
+    fits = (
+        elems == LANES and spans == 2 * zdev and planes == zdev == 4
+        and walls == planes * 2 * LANES and q % 16 == 1 and q < LANES
+    )
+    if fits:
+        return kernels_on_device(spans, planes, *args)
+    return on_device(*args)
+
+
 def solution(mesh):
     placed = (
         P(None, "span", None, "plane"),
@@ -135,7 +591,7 @@
         P("span", None),
     )
     return jax.shard_map(
-        on_device,
+        functools.partial(chosen, mesh.shape["span"], mesh.shape["plane"]),
         mesh=mesh,
         in_specs=placed,
         out_specs=(P(None, "span", None, "plane"), P("span", "plane")),

time: 299 us -> 97.6 us (0.33); the launches traced: 294 us -> 97.3 us
  Pallas kernels: 0 us -> 87.1 us
  blocking collectives: 77.4 us -> 0 us
  local copies, waits for them, and re-layouts: 79.6 us -> 9.58 us
  matrix products: 48.8 us -> 0 us
  waiting for transfers between devices: 38.8 us -> 0 us
  between operations: 21.1 us -> 0.68 us
  starting transfers between devices: 17.6 us -> 0 us
  other arithmetic: 11 us -> 0 us
    pallas_call x0 -> x3, Pallas kernels: none -> 87.1 us  [the longest x1 39.4 us: kernels_on_device(): pl.pallas_call(functools.partial(enter_kernel, spans, planes, zdev, q, qp...]
    dot_general x15 -> x0, matrix products: 48.8 us -> none  [the longest x3 17 us: transport(): jnp.einsum('ai,czibe->czabe', matrix, shaped, precision=HIGHEST)]
    psum x1 -> x0, blocking collectives: 39.5 us -> none  [on_device(): square_total = lax.psum(jnp.sum(grad_share * grad_share), ('span', 'plane'))]
    all_gather x1 -> x0, blocking collectives: 38 us -> none  [on_device(): all_modes = lax.all_gather(helmholtz_inverse, 'span', axis=0, tiled=True)]
    reshape x9 -> x0, local copies, waits for them, and re-layouts: 26.1 us -> none  [the longest x2 12 us: transport(): field_data.reshape(field_data.shape[0], field_data.shape[1], side_nodes,...]
    unnamed x2 -> x0, waiting for transfers between devices: 20.6 us -> none
    all_to_all x3 -> x0, waiting for transfers between devices: 18.2 us -> none  [the longest x1 18.2 us: to_plane_layout(): lax.all_to_all(point_data, 'span', split_axis=1, concat_axis=3, tiled=True)]
    all_to_all x3 -> x0, starting transfers between devices: 17.4 us -> none  [the longest x1 7.31 us: on_device(): lax.all_to_all(adjoint, 'span', split_axis=3, concat_axis=1, tiled=True)]
  transfers between devices with their start and end apart: 4 -> 0, of which waited for: 2 -> 0; matrix products, arithmetic and copies ran while one was open for 14% -> 0% of each run, Pallas kernels for 0% -> 0%
where the time goes in v2:
time: 97.6 us; the launch traced here: 97.3 us
  Pallas kernels  87.1 us (89%)
  local copies, waits for them, and re-layouts  9.58 us (10%)
    pallas_call x1, Pallas kernels, kernels_on_device(): pl.pallas_call(functools.partial(enter_kernel, spans, planes, zdev, q, qp...  39.4 us
    pallas_call x1, Pallas kernels, kernels_on_device(): pl.pallas_call(functools.partial(leave_kernel, spans, planes, zdev, q, fl...  27.6 us
    pallas_call x1, Pallas kernels, kernels_on_device(): pl.pallas_call(functools.partial(steps_kernel, spans, planes, zdev, qp),...  20 us
    unnamed x14, local copies, waits for them, and re-layouts  6.93 us
    pallas_call x1, local copies, waits for them, and re-layouts, kernels_on_device(): pl.pallas_call(functools.partial(leave_kernel, spans, planes, zdev, q, fl...  1.96 us

profile of v2, /device:TPU:0, one launch (start us, length us, event | category | flops | bytes accessed | tf_op | source)
XLA Modules:
  0.0 97.3 jit_solution(1946396855976898066)
XLA Ops:
  0.6 0.0 copy-start
  0.6 0.0 copy-start.1
  0.6 2.7 %copy.15.ck_ref = bf16[8,2,4,81,128]{4,3,2,1,0:T(8,128)(2,1)} copy(bf16[8,2,4,81,128]{4,2,3,1,0:T(4,128)(2,1)} %param.12) | data formatting | bytes 2654208 | tf_op args[1]
  3.4 0.0 copy-done
  3.4 0.9 copy.14.adj_ref
  4.2 0.0 copy-done.1
  4.2 0.0 copy-start.2
  4.3 0.7 pad.4.inv_ref
  4.9 0.0 copy-start.3
  4.9 39.4 %enter.1 = (f32[96,1536]{1,0:T(8,128)}, f32[3,2,96,512]{3,2,1,0:T(8,128)}, f32[4,8,96,128]{3,2,1,0:T(8,128)}) custom-call(s32[3]{0:T(128)} %step_ref.1, f32[3,4,81,128]{3,2,1,0:T(8,128)} %copy.14.adj_ref, bf16[8,2,4,81,128]{4,3,2,1,0:T(8,128)(2,1)} %copy.15.ck_ref, f32[4,96,128]{2,1,0:T(8,128)} %pad.4.inv_ref), custom_call_target="tpu_custom_call" | custom-call | tf_op jit(solution)/shard_map/enter/pallas_call | solution.py:512
  44.4 0.0 copy-done.2
  44.4 1.0 %copy.16.elem_ref = s32[1024,2]{1,0:T(8,128)} copy(s32[1024,2]{0,1:T(2,128)S(1)} %copy-done.2) | data formatting | bytes 16384 | tf_op args[5]
  45.5 0.0 copy-done.3
  45.5 1.0 %copy.17.local_ref = s32[1024,2]{1,0:T(8,128)} copy(s32[1024,2]{0,1:T(2,128)S(1)} %copy-done.3) | data formatting | bytes 16384 | tf_op args[6]
  46.5 20.0 %steps.1 = (f32[96,1536]{1,0:T(8,128)}, f32[8,4,8,128]{3,2,1,0:T(8,128)}) custom-call(f32[96,1536]{1,0:T(8,128)} %get-tuple-element.7.xs_ref, f32[3,2,96,512]{3,2,1,0:T(8,128)} %get-tuple-element.8.vs_ref, f32[4,8,96,128]{3,2,1,0:T(8,128)} %get-tuple-element.9.modes_ref, f32[2,128]{1,0:T(2,128)} %metric_ref.1, s32[1024,2]{1,0:T(8,128)} %copy.16.elem_ref, ...), custom_call_target="tpu_custom_call" | custom-call | tf_op jit(solution)/shard_map/steps/pallas_call | solution.py:531
  66.5 27.6 %leave.1 = (f32[3,4,81,128]{3,2,1,0:T(8,128)}, f32[4,256]{1,0:T(4,128)}) custom-call(f32[96,1536]{1,0:T(8,128)} %get-tuple-element.10.xs_ref, f32[8,4,8,128]{3,2,1,0:T(8,128)} %get-tuple-element.11.wall_ref, f32[4,1024]{1,0:T(4,128)} %weight_ref.1), custom_call_target="tpu_custom_call" | custom-call | tf_op jit(solution)/shard_map/leave/pallas_call | solution.py:546
  94.1 2.0 %copy.18 = f32[3,4,81,128]{3,1,2,0:T(4,128)} copy(f32[3,4,81,128]{3,2,1,0:T(8,128)} %get-tuple-element.12) | data formatting | bytes 995328 | tf_op jit(solution)/shard_map/leave/pallas_call | solution.py:546
  96.1 1.3 %copy.20 = f32[4,256]{1,0:T(4,128)} copy(f32[4,256]{1,0:T(4,128)} %get-tuple-element.17) | data formatting | bytes 8192
  (1 shorter events, 0.0 us)
Async XLA Ops:
  0.6 2.7 %copy-start = (f32[3,4,81,128]{3,1,2,0:T(4,128)S(1)}, f32[3,4,81,128]{3,1,2,0:T(4,128)}, u32[]{:S(2)}) copy-start(f32[3,4,81,128]{3,1,2,0:T(4,128)} %param.11) | copy-start | bytes 1492996
  0.6 3.6 %copy-start.1 = (f32[4,81,81]{2,0,1:T(4,128)S(1)}, f32[4,81,81]{2,0,1:T(4,128)}, u32[]{:S(2)}) copy-start(f32[4,81,81]{2,0,1:T(4,128)} %param.15) | copy-start | bytes 314932
  4.2 40.2 %copy-start.2 = (s32[1024,2]{0,1:T(2,128)S(1)}, s32[1024,2]{0,1:T(2,128)}, u32[]{:S(2)}) copy-start(s32[1024,2]{0,1:T(2,128)} %param.16) | copy-start | bytes 24580
  4.9 40.5 %copy-start.3 = (s32[1024,2]{0,1:T(2,128)S(1)}, s32[1024,2]{0,1:T(2,128)}, u32[]{:S(2)}) copy-start(s32[1024,2]{0,1:T(2,128)} %param.17) | copy-start | bytes 24580

commit v3 on v2

--- a/solution.py
+++ b/solution.py
@@ -169,10 +169,13 @@
     )
 
 
-def enter_kernel(spans, planes, zdev, q, qp,
-                 step_ref, adj_ref, ck_ref, inv_ref,
-                 xs_ref, vs_ref, modes_ref,
-                 tail, snd, rcv, vsnd, vrcv, sems, local_sem):
+def step_kernel(spans, planes, zdev, q, qp,
+                step_ref, adj_ref, ck_ref, inv_ref, metric_ref, elem_ref, local_ref, weight_ref,
+                basis_ref, diff_ref, place_ref,
+                back, weighted_ref, trcv,
+                xs_ref, vs_ref, modes_ref, tail, snd, rcv, vsnd, vrcv,
+                coef, solved, product, modes_hi, modes_lo, bsnd,
+                wall, rows_in, part, wrcv, square, srcv, total, sems, local_sem):
     share = LANES // spans
     me, p = lax.axis_index("span"), lax.axis_index("plane")
     bulk = q - 1
@@ -222,7 +225,7 @@
     parts = swap_blocks([tail[g] for g in range(spans)], share)
     for d in range(spans):
         snd[d, sets * half:, :] = parts[d]
-    fields, speeds = [], []
+    fields, speeds = [], [[] for _ in range(NSTEP)]
     for o in range(1, spans):
         to, s = (me + o) % spans, (me + spans - o) % spans
         out = remote(snd.at[to], rcv.at[me], sems, 4, o, span_to(o))
@@ -230,17 +233,18 @@
         fields.append((out, remote(snd.at[to], rcv.at[s], sems, 4, o, span_to(o))))
     own = pltpu.make_async_copy(snd.at[me], rcv.at[me], local_sem.at[0])
     own.start()
+    wide = zdev * LANES
     for t in range(NSTEP):
         slot = step_ref[t]
         parts = [ck_ref[slot, k // zdev, k % zdev].astype(F32)[:bulk] for k in range(2 * zdev)]
         parts = swap_blocks(parts, share)
         for d in range(spans):
             vsnd[d, t] = parts[d].astype(BF16)
-    for o in range(1, spans):
-        to, s = (me + o) % spans, (me + spans - o) % spans
-        out = remote(vsnd.at[to], vrcv.at[me], sems, 5, o, span_to(o))
-        out.start()
-        speeds.append((out, remote(vsnd.at[to], vrcv.at[s], sems, 5, o, span_to(o))))
+        for o in range(1, spans):
+            to, s = (me + o) % spans, (me + spans - o) % spans
+            out = remote(vsnd.at[to, t], vrcv.at[me, t], sems, 5 + t, o, span_to(o))
+            out.start()
+            speeds[t].append((out, remote(vsnd.at[to, t], vrcv.at[s, t], sems, 5 + t, o, span_to(o))))
     vown = pltpu.make_async_copy(vsnd.at[me], vrcv.at[me], local_sem.at[1])
     vown.start()
     mine = [pltpu.make_async_copy(inv_ref.at[j], modes_ref.at[j, me], local_sem.at[2 + j])
@@ -249,6 +253,17 @@
         c.start()
     xs_ref[bulk:, :] = jnp.zeros_like(xs_ref[bulk:, :])
     vs_ref[:, :, bulk:, :] = jnp.zeros_like(vs_ref[:, :, bulk:, :])
+    product[...] = jnp.zeros_like(product)
+    lane = lax.broadcasted_iota(jnp.int32, (1, LANES), 1)
+    rolled = pltpu.roll(metric_ref[...], (LANES - me * share) % LANES, 1)
+    scale = jnp.where(lane < share, rolled, 0.0)
+    k = share
+    while k < LANES:
+        scale = scale + pltpu.roll(scale, k, 1)
+        k *= 2
+    block = lax.broadcasted_iota(jnp.int32, (1, 3 * LANES), 1) % LANES // share
+    first = jnp.concatenate([scale[0:1]] * zdev, axis=1)
+    second = jnp.concatenate([scale[1:2]] * zdev, axis=1)
 
     for o in range(spans - 1):
         stage1[o][1].wait_recv()
@@ -274,125 +289,46 @@
             z = k % zdev
             vs_ref[t, k // zdev, bulk:q, z * LANES:(z + 1) * LANES] = parts[k][2 + t:3 + t]
     vown.wait()
-    for c in speeds:
-        c[1].wait_recv()
+
     for t in range(NSTEP):
+        for c in speeds[t]:
+            c[1].wait_recv()
         parts = swap_blocks([vrcv[s, t].astype(F32) for s in range(spans)], share)
         for k in range(2 * zdev):
             z = k % zdev
             vs_ref[t, k // zdev, :bulk, z * LANES:(z + 1) * LANES] = parts[k]
-    for c in mine:
-        c.wait()
-    for group in (stage2c, stage3):
-        for c in group:
-            c[1].wait_recv()
-    for group in (stage1, stage2x, stage2c, stage3, fields, speeds):
-        for c in group:
-            c[0].wait_send()
-
-
-def split(x):
-    high = x.astype(BF16)
-    return high, (x - high.astype(F32)).astype(BF16)
-
-
-def mul3(a, b, dims=((1,), (0,))):
-    def one(x, y):
-        return lax.dot_general(x, y, (dims, ((), ())), preferred_element_type=F32)
-    return one(a[0], b[0]) + (one(a[0], b[1]) + one(a[1], b[0]))
-
-
-def steps_kernel(spans, planes, zdev, qp,
-                 xs_ref, vs_ref, modes_ref, metric_ref, elem_ref, local_ref,
-                 basis_ref, diff_ref, place_ref,
-                 out_ref, wall_ref,
-                 field, coef, solved, product, modes_hi, modes_lo):
-    share = LANES // spans
-    wide = zdev * LANES
-    me, p = lax.axis_index("span"), lax.axis_index("plane")
-    lane = lax.broadcasted_iota(jnp.int32, (1, LANES), 1)
-    rolled = pltpu.roll(metric_ref[...], (LANES - me * share) % LANES, 1)
-    scale = jnp.where(lane < share, rolled, 0.0)
-    k = share
-    while k < LANES:
-        scale = scale + pltpu.roll(scale, k, 1)
-        k *= 2
-    for j in range(zdev):
-        for s in range(spans):
-            high, low = split(modes_ref[j, s])
-            modes_hi[j, s * qp:(s + 1) * qp, :] = high
-            modes_lo[j, s * qp:(s + 1) * qp, :] = low
-    field[...] = xs_ref[...]
-    product[...] = jnp.zeros_like(product)
-    block = lax.broadcasted_iota(jnp.int32, (1, 3 * LANES), 1) % LANES // share
-    first = jnp.concatenate([scale[0:1]] * zdev, axis=1)
-    second = jnp.concatenate([scale[1:2]] * zdev, axis=1)
-
-    def one_step(t, carry):
         v0 = vs_ref[t, 0] * first
         v1 = vs_ref[t, 1] * second
         for c in range(3):
-            x = field[:, c * wide:(c + 1) * wide]
+            x = xs_ref[:, c * wide:(c + 1) * wide]
             d = mul3((diff_ref[0], diff_ref[1]), split(x))
             coef[c * qp:(c + 1) * qp, :] = x + v0 * d[:qp] + v1 * d[qp:]
         y = mul3(split(coef[...]), (basis_ref[0], basis_ref[1]))
         coef[...] = y
+        if t == 0:
+            for c in mine:
+                c.wait()
+            for group in (stage2c, stage3):
+                for c in group:
+                    c[1].wait_recv()
+            for j in range(zdev):
+                for s in range(spans):
+                    high, low = split(modes_ref[j, s])
+                    modes_hi[j, s * qp:(s + 1) * qp, :] = high
+                    modes_lo[j, s * qp:(s + 1) * qp, :] = low
         for j in range(zdev):
             lanes = slice(j * LANES, (j + 1) * LANES)
             x = jnp.concatenate([coef[c * qp:(c + 1) * qp, lanes] for c in range(3)], axis=1)
             r = mul3((modes_hi[j, :, :qp], modes_lo[j, :, :qp]), split(x))
-            total = r[:qp]
+            acc = r[:qp]
             for s in range(1, spans):
-                total = jnp.where(block == s, r[s * qp:(s + 1) * qp], total)
+                acc = jnp.where(block == s, r[s * qp:(s + 1) * qp], acc)
             for c in range(3):
-                solved[c * qp:(c + 1) * qp, lanes] = total[:, c * LANES:(c + 1) * LANES]
+                solved[c * qp:(c + 1) * qp, lanes] = acc[:, c * LANES:(c + 1) * LANES]
         y = mul3(split(solved[...]), (basis_ref[0], basis_ref[1]), ((1,), (1,)))
         for c in range(3):
-            field[:, c * wide:(c + 1) * wide] = y[c * qp:(c + 1) * qp]
+            xs_ref[:, c * wide:(c + 1) * wide] = y[c * qp:(c + 1) * qp]
         product[...] += y[qp:2 * qp] * vs_ref[t, 1]
-        return carry
-
-    lax.fori_loop(0, NSTEP, one_step, 0)
-    out_ref[...] = field[...]
-
-    high, low = split(product[...])
-    base = p * LANES + me * share
-    mode = lax.broadcasted_iota(jnp.int32, (1, qp), 1)
-    near = lane % share
-
-    def picked(row):
-        total = 0.0
-        for k in range(2):
-            pick = jnp.where(local_ref[pl.ds(row, LANES), k:k + 1] == mode, 1.0, 0.0).astype(BF16)
-            keep = elem_ref[pl.ds(row, LANES), k:k + 1] - base == near
-            keep = jnp.concatenate([jnp.where(keep, 1.0, 0.0)] * zdev, axis=1)
-            got = jnp.dot(pick, high, preferred_element_type=F32)
-            got = got + jnp.dot(pick, low, preferred_element_type=F32)
-            total = total + got * keep
-        return split(total)
-
-    for part in range(planes):
-        total = 0.0
-        for h in range(2):
-            pair = picked((part * 2 + h) * LANES)
-            for v in pair:
-                total = total + lax.dot_general(
-                    place_ref[h], v, (((1,), (1,)), ((), ())), preferred_element_type=F32)
-        for s in range(spans):
-            wall_ref[s, part] = total[s * 8:(s + 1) * 8]
-
-
-def leave_kernel(spans, planes, zdev, q, count,
-                 xs_ref, wall_ref, weight_ref,
-                 out_ref, grad_ref,
-                 tail, snd, rcv, wrcv, part, prcv, square, srcv, total, trcv, sems, local_sem):
-    share = LANES // spans
-    me, p = lax.axis_index("span"), lax.axis_index("plane")
-    bulk = q - 1
-    half = bulk // 2
-    slabs = 3 * zdev
-    sets = 2 * slabs // spans
-    greet(spans, planes)
 
     def exchange(kind, size, axis, pick_src, dst):
         at = lax.axis_index(axis)
@@ -404,10 +340,30 @@
             pairs.append((out, remote(pick_src(to), dst.at[s], sems, kind, o, {axis: to})))
         return pairs
 
-    walls = exchange(0, spans, "span", lambda to: wall_ref.at[to], wrcv)
-    wown = pltpu.make_async_copy(wall_ref.at[me], wrcv.at[me], local_sem.at[0])
-    wown.start()
-    tail[...] = jnp.zeros_like(tail)
+    high, low = split(product[...].T)
+    base = p * LANES + me * share
+    mode = lax.broadcasted_iota(jnp.int32, (qp, LANES), 0)
+    near = lax.broadcasted_iota(jnp.int32, (LANES, LANES), 0) % share + base
+    for piece in range(planes):
+        acc = 0.0
+        for h in range(2):
+            lo = (piece * 2 + h) * LANES
+            got = 0.0
+            for k in range(2):
+                pick = jnp.where(local_ref[k:k + 1, lo:lo + LANES] == mode, 1.0, 0.0).astype(BF16)
+                keep = jnp.where(elem_ref[k:k + 1, lo:lo + LANES] == near, 1.0, 0.0)
+                keep = jnp.concatenate([keep] * zdev, axis=0)
+                one = jnp.dot(high, pick, preferred_element_type=F32)
+                one = one + jnp.dot(low, pick, preferred_element_type=F32)
+                got = got + one * keep
+            for v in split(got):
+                acc = acc + jnp.dot(place_ref[h], v, preferred_element_type=F32)
+        for s in range(spans):
+            wall[piece, s] = acc[s * 8:(s + 1) * 8]
+    rows = exchange(8, planes, "plane", lambda to: wall.at[to], rows_in)
+    rown = pltpu.make_async_copy(wall.at[p], rows_in.at[p], local_sem.at[0])
+    rown.start()
+
     for k in range(slabs):
         tail[k % spans, k // spans:k // spans + 1, :] = xs_ref[bulk:q, k * LANES:(k + 1) * LANES]
     for i in range(sets):
@@ -418,57 +374,75 @@
             parts.append(xs_ref[r:r + half, k * LANES:(k + 1) * LANES])
         parts = swap_blocks(parts, share)
         for d in range(spans):
-            snd[d, i * half:(i + 1) * half, :] = parts[d]
+            bsnd[d, i * half:(i + 1) * half, :] = parts[d]
     parts = swap_blocks([tail[g] for g in range(spans)], share)
     for d in range(spans):
-        snd[d, sets * half:, :] = parts[d]
-    fields = exchange(1, spans, "span", lambda to: snd.at[to], rcv)
-    own = pltpu.make_async_copy(snd.at[me], rcv.at[me], local_sem.at[1])
-    own.start()
-
+        bsnd[d, sets * half:, :] = parts[d]
+    rown.wait()
+    for c in rows:
+        c[1].wait_recv()
+    part[...] = sum(rows_in[s] for s in range(planes))
+    walls = exchange(9, spans, "span", lambda to: part.at[to], wrcv)
+    returned = exchange(10, spans, "span", lambda to: bsnd.at[to], back)
+    bown = pltpu.make_async_copy(bsnd.at[me], back.at[me], local_sem.at[1])
+    bown.start()
+    wown = pltpu.make_async_copy(part.at[me], wrcv.at[me], local_sem.at[0])
+    wown.start()
     wown.wait()
     for c in walls:
         c[1].wait_recv()
-    part[...] = sum(wrcv[s] for s in range(spans))
-    rows = exchange(2, planes, "plane", lambda to: part.at[to], prcv)
-    pown = pltpu.make_async_copy(part.at[p], prcv.at[p], local_sem.at[2])
-    pown.start()
-    pown.wait()
-    for c in rows:
-        c[1].wait_recv()
-    block = sum(prcv[s] for s in range(planes))
-    sums = jnp.concatenate([block[:zdev], block[zdev:]], axis=1)
+    both = sum(wrcv[s] for s in range(spans))
+    sums = jnp.concatenate([both[:zdev], both[zdev:]], axis=1)
     weight = weight_ref[:, pl.ds(pl.multiple_of(p * 2 * LANES, 2 * LANES), 2 * LANES)]
     weighted = weight * sums
+    weighted_ref[...] = weighted
     sq = weighted * weighted
     square[...] = jnp.broadcast_to(jnp.sum(sq[:, :LANES] + sq[:, LANES:], axis=0, keepdims=True), (8, LANES))
-    squares = exchange(3, spans, "span", lambda to: square, srcv)
+    squares = exchange(11, spans, "span", lambda to: square, srcv)
     srcv[me] = square[...]
     for c in squares:
         c[1].wait_recv()
     total[...] = sum(srcv[s] for s in range(spans))
-    totals = exchange(4, planes, "plane", lambda to: total, trcv)
+    totals = exchange(12, planes, "plane", lambda to: total, trcv)
     trcv[p] = total[...]
     for c in totals:
         c[1].wait_recv()
+    bown.wait()
+    for c in returned:
+        c[1].wait_recv()
+    for group in (stage1, stage2x, stage2c, stage3, fields, *speeds, rows, walls, returned, squares, totals):
+        for c in group:
+            c[0].wait_send()
+
+
+def split(x):
+    high = x.astype(BF16)
+    return high, (x - high.astype(F32)).astype(BF16)
+
+
+def mul3(a, b, dims=((1,), (0,))):
+    def one(x, y):
+        return lax.dot_general(x, y, (dims, ((), ())), preferred_element_type=F32)
+    return one(a[0], b[0]) + (one(a[0], b[1]) + one(a[1], b[0]))
+
+
+def finish_kernel(spans, planes, zdev, q, count, back, weighted_ref, trcv, out_ref, grad_ref):
+    share = LANES // spans
+    bulk = q - 1
+    half = bulk // 2
+    slabs = 3 * zdev
+    sets = 2 * slabs // spans
     full = jnp.sum(sum(trcv[s] for s in range(planes))[0:1], axis=1, keepdims=True)
-    grad_ref[...] = weighted * lax.rsqrt(full / count + 1e-06)
-
-    own.wait()
-    for c in fields:
-        c[1].wait_recv()
+    grad_ref[...] = weighted_ref[...] * lax.rsqrt(full / count + 1e-06)
     for i in range(sets):
-        parts = swap_blocks([rcv[s, i * half:(i + 1) * half, :] for s in range(spans)], share)
+        parts = swap_blocks([back[s, i * half:(i + 1) * half, :] for s in range(spans)], share)
         for g in range(spans):
             h = spans * i + g
             k, r = h // 2, (h % 2) * half
-            out_ref[k // zdev, k % zdev, r:r + half, :] = parts[g]
-    parts = swap_blocks([rcv[s, sets * half:, :] for s in range(spans)], share)
+            out_ref[k // zdev, r:r + half, k % zdev, :] = parts[g]
+    parts = swap_blocks([back[s, sets * half:, :] for s in range(spans)], share)
     for k in range(slabs):
-        out_ref[k // zdev, k % zdev, bulk:q, :] = parts[k % spans][k // spans:k // spans + 1]
-    for group in (walls, fields, rows, squares, totals):
-        for c in group:
-            c[0].wait_send()
+        out_ref[k // zdev, bulk:q, k % zdev, :] = parts[k % spans][k // spans:k // spans + 1]
 
 
 def halves(table):
@@ -509,62 +483,50 @@
     rows = 3 * zdev * bulk // spans + 8
     inverse = jnp.pad(helmholtz_inverse, ((0, 0), (0, qp - q), (0, LANES - q)))
     shape = jax.ShapeDtypeStruct
-    field, speed, modes = pl.pallas_call(
-        functools.partial(enter_kernel, spans, planes, zdev, q, qp),
-        out_shape=(shape((qp, 3 * wide), F32), shape((NSTEP, 2, qp, wide), F32),
-                   shape((zdev, spans, qp, LANES), F32)),
-        in_specs=[pl.BlockSpec(memory_space=pltpu.SMEM)] + vmem(3),
+    basis, diff, place = tables(spans, zdev, q, qp)
+    back, weighted, squares = pl.pallas_call(
+        functools.partial(step_kernel, spans, planes, zdev, q, qp),
+        out_shape=(shape((spans, rows, LANES), F32), shape((zdev, wall_count // planes), F32),
+                   shape((planes, 8, LANES), F32)),
+        in_specs=[pl.BlockSpec(memory_space=pltpu.SMEM)] + vmem(10),
         out_specs=tuple(vmem(3)),
         scratch_shapes=[
+            pltpu.VMEM((qp, 3 * wide), F32),
+            pltpu.VMEM((NSTEP, 2, qp, wide), F32),
+            pltpu.VMEM((zdev, spans, qp, LANES), F32),
             pltpu.VMEM((spans, 8, LANES), F32),
             pltpu.VMEM((spans, rows, LANES), F32),
             pltpu.VMEM((spans, rows, LANES), F32),
             pltpu.VMEM((spans, NSTEP, bulk, LANES), BF16),
             pltpu.VMEM((spans, NSTEP, bulk, LANES), BF16),
-            pltpu.SemaphoreType.DMA((2, 6, spans)),
-            pltpu.SemaphoreType.DMA((2 + zdev,)),
-        ],
-        compiler_params=pltpu.CompilerParams(collective_id=0, has_side_effects=True),
-        name="enter",
-    )(checkpoint_step, adjoint, checkpoints, inverse)
-    basis, diff, place = tables(spans, zdev, q, qp)
-    field, walls = pl.pallas_call(
-        functools.partial(steps_kernel, spans, planes, zdev, qp),
-        out_shape=(shape((qp, 3 * wide), F32), shape((spans, planes, 8, LANES), F32)),
-        in_specs=vmem(9),
-        out_specs=tuple(vmem(2)),
-        scratch_shapes=[
-            pltpu.VMEM((qp, 3 * wide), F32),
             pltpu.VMEM((3 * qp, wide), F32),
             pltpu.VMEM((3 * qp, wide), F32),
             pltpu.VMEM((qp, wide), F32),
             pltpu.VMEM((zdev, spans * qp, LANES), BF16),
             pltpu.VMEM((zdev, spans * qp, LANES), BF16),
-        ],
-        name="steps",
-    )(field, speed, modes, metric, wall_element, wall_local, basis, diff, place)
-    return pl.pallas_call(
-        functools.partial(leave_kernel, spans, planes, zdev, q, float(spans * zdev * wall_count)),
-        out_shape=(shape(adjoint.shape, F32), shape((zdev, wall_count // planes), F32)),
-        in_specs=vmem(3),
-        out_specs=tuple(vmem(2)),
-        scratch_shapes=[
+            pltpu.VMEM((spans, rows, LANES), F32),
+            pltpu.VMEM((planes, spans, 8, LANES), F32),
+            pltpu.VMEM((planes, spans, 8, LANES), F32),
             pltpu.VMEM((spans, 8, LANES), F32),
-            pltpu.VMEM((spans, rows, LANES), F32),
-            pltpu.VMEM((spans, rows, LANES), F32),
-            pltpu.VMEM((spans, planes, 8, LANES), F32),
-            pltpu.VMEM((planes, 8, LANES), F32),
-            pltpu.VMEM((planes, 8, LANES), F32),
+            pltpu.VMEM((spans, 8, LANES), F32),
             pltpu.VMEM((8, LANES), F32),
             pltpu.VMEM((spans, 8, LANES), F32),
             pltpu.VMEM((8, LANES), F32),
-            pltpu.VMEM((planes, 8, LANES), F32),
-            pltpu.SemaphoreType.DMA((2, 5, spans)),
-            pltpu.SemaphoreType.DMA((3,)),
+            pltpu.SemaphoreType.DMA((2, 13, spans)),
+            pltpu.SemaphoreType.DMA((2 + zdev,)),
         ],
-        compiler_params=pltpu.CompilerParams(collective_id=1, has_side_effects=True),
-        name="leave",
-    )(field, walls, wall_weight)
+        compiler_params=pltpu.CompilerParams(collective_id=0, has_side_effects=True),
+        name="steps",
+    )(checkpoint_step, adjoint, checkpoints, inverse, metric, wall_element.T, wall_local.T,
+      wall_weight, basis, diff, place)
+    field, gradient = pl.pallas_call(
+        functools.partial(finish_kernel, spans, planes, zdev, q, float(spans * zdev * wall_count)),
+        out_shape=(shape((3, q, zdev, LANES), F32), shape((zdev, wall_count // planes), F32)),
+        in_specs=vmem(3),
+        out_specs=tuple(vmem(2)),
+        name="finish",
+    )(back, weighted, squares)
+    return field.transpose(0, 2, 1, 3), gradient
 
 
 def chosen(spans, planes, *args):

time: 97.6 us -> 84.6 us (0.87)
  Pallas kernels: 87.1 us -> 78.8 us
  local copies, waits for them, and re-layouts: 9.58 us -> 5.01 us
    pallas_call x3 -> x2, Pallas kernels: 87.1 us -> 78.8 us  [the longest x1 76.1 us: kernels_on_device(): pl.pallas_call(functools.partial(step_kernel, spans, planes, zdev, q, qp)...]
    unnamed x14 -> x5, local copies, waits for them, and re-layouts: 6.93 us -> 4.31 us
    pallas_call x1 -> x0, local copies, waits for them, and re-layouts: 1.96 us -> none  [kernels_on_device(): pl.pallas_call(functools.partial(leave_kernel, spans, planes, zdev, q, fl...]
where the time goes in v3:
time: 84.6 us; the launch traced here: 84.4 us
  Pallas kernels  78.8 us (93%)
  local copies, waits for them, and re-layouts  5.01 us (6%)
    pallas_call x1, Pallas kernels, kernels_on_device(): pl.pallas_call(functools.partial(step_kernel, spans, planes, zdev, q, qp)...  76.1 us
    unnamed x5, local copies, waits for them, and re-layouts  4.31 us
    pallas_call x1, Pallas kernels, kernels_on_device(): pl.pallas_call(functools.partial(finish_kernel, spans, planes, zdev, q, f...  2.66 us

profile of v3, /device:TPU:0, one launch (start us, length us, event | category | flops | bytes accessed | tf_op | source)
XLA Modules:
  0.0 84.4 jit_solution(9073138488214150987)
XLA Ops:
  0.6 0.0 copy-start
  0.6 1.0 %copy.13 = f32[4,81,81]{2,1,0:T(8,128)S(1)} copy(f32[4,81,81]{2,0,1:T(4,128)} %param.15) | data formatting | bytes 209952 | tf_op args[4]
  1.7 0.7 pad.4.inv_ref
  2.4 1.9 %copy.14.adj_ref = f32[3,4,81,128]{3,2,1,0:T(8,128)} copy(f32[3,4,81,128]{3,1,2,0:T(4,128)} %param.11) | data formatting | bytes 995328 | tf_op args[0]
  4.3 0.0 copy-done
  4.3 1.4 %copy.15.ck_ref = bf16[8,2,4,81,128]{4,3,2,1,0:T(8,128)(2,1)} copy(bf16[8,2,4,81,128]{4,2,3,1,0:T(4,128)(2,1)S(1)} %copy-done) | data formatting | bytes 2654208 | tf_op args[1]
  5.6 76.1 %steps.1 = (f32[8,128,128]{2,1,0:T(8,128)}, f32[4,256]{1,0:T(4,128)}, f32[4,8,128]{2,1,0:T(8,128)}) custom-call(s32[3]{0:T(128)} %step_ref.1, f32[3,4,81,128]{3,2,1,0:T(8,128)} %copy.14.adj_ref, bf16[8,2,4,81,128]{4,3,2,1,0:T(8,128)(2,1)} %copy.15.ck_ref, f32[4,96,128]{2,1,0:T(8,128)} %pad.4.inv_ref, f32[2,128]{1,0:T(2,128)} %metric_ref.1, ...), custom_call_target="tpu_custom_call" | custom-call | tf_op jit(solution)/shard_map/steps/pallas_call | solution.py:487
  81.8 2.7 %finish.1 = (f32[3,81,4,128]{3,2,1,0:T(4,128)}, f32[4,256]{1,0:T(4,128)}) custom-call(f32[8,128,128]{2,1,0:T(8,128)} %get-tuple-element.7.back, f32[4,256]{1,0:T(4,128)} %get-tuple-element.8.weighted_ref, f32[4,8,128]{2,1,0:T(8,128)} %get-tuple-element.9.trcv), custom_call_target="tpu_custom_call" | custom-call | tf_op jit(solution)/shard_map/finish/pallas_call | solution.py:522
Async XLA Ops:
  0.6 3.6 %copy-start = (bf16[8,2,4,81,128]{4,2,3,1,0:T(4,128)(2,1)S(1)}, bf16[8,2,4,81,128]{4,2,3,1,0:T(4,128)(2,1)}, u32[]{:S(2)}) copy-start(bf16[8,2,4,81,128]{4,2,3,1,0:T(4,128)(2,1)} %param.12) | copy-start | bytes 3981316

commit v4 on v3

--- a/solution.py
+++ b/solution.py
@@ -152,6 +152,21 @@
     return parts
 
 
+def coded(x):
+    top = jnp.maximum(jnp.max(jnp.abs(x), axis=0, keepdims=True), 1e-30)
+    return jnp.round(x * (32767.0 / top)).astype(jnp.int32), top * (1.0 / 32767.0)
+
+
+def coded_blocks(rows, sets, half):
+    pairs = [coded(rows[i * half:(i + 1) * half]) for i in range(sets)]
+    whole = jnp.concatenate([a for a, _ in pairs], axis=0)
+    return whole.astype(jnp.int16), [b for _, b in pairs]
+
+
+def decoded(x, scale):
+    return x.astype(jnp.int32).astype(F32) * scale
+
+
 def greet(spans, planes):
     me, p = lax.axis_index("span"), lax.axis_index("plane")
     barrier = pltpu.get_barrier_semaphore()
@@ -172,9 +187,9 @@
 def step_kernel(spans, planes, zdev, q, qp,
                 step_ref, adj_ref, ck_ref, inv_ref, metric_ref, elem_ref, local_ref, weight_ref,
                 basis_ref, diff_ref, place_ref,
-                back, weighted_ref, trcv,
-                xs_ref, vs_ref, modes_ref, tail, snd, rcv, vsnd, vrcv,
-                coef, solved, product, modes_hi, modes_lo, bsnd,
+                back, tback, weighted_ref, trcv,
+                xs_ref, vs_ref, padded, inv16, modes_ref, tail, stage, snd, tsnd, rcv, trc, vsnd, vrcv,
+                coef, solved, product, modes_hi, modes_lo, bsnd, tbsnd,
                 wall, rows_in, part, wrcv, square, srcv, total, sems, local_sem):
     share = LANES // spans
     me, p = lax.axis_index("span"), lax.axis_index("plane")
@@ -187,6 +202,16 @@
     def span_to(o):
         return {"span": (me + o) % spans}
 
+    eye = (lax.broadcasted_iota(jnp.int32, (qp, LANES), 0)
+           == lax.broadcasted_iota(jnp.int32, (qp, LANES), 1))
+    padded[...] = jnp.zeros_like(padded)
+    extra = []
+    for j in range(zdev):
+        padded[:q, :q] = inv_ref[:, j, :]
+        x = padded[...]
+        whole, scale = coded(jnp.where(eye, 0.0, x))
+        inv16[j] = whole.astype(jnp.int16)
+        extra.append((scale, jnp.sum(jnp.where(eye, x, 0.0), axis=0, keepdims=True)))
     xpeer = {"plane": (p + 2) % planes}
     cpeer = {"plane": p + 1 - 2 * (p % 2)}
     px = (p + 2) % planes
@@ -195,9 +220,9 @@
     stage1, stage2x, stage2c, stage3 = [], [], [], []
     for o in range(1, spans):
         s = (me + spans - o) % spans
-        out = remote(inv_ref.at[p], modes_ref.at[p, me], sems, 0, o, span_to(o))
+        out = remote(inv16.at[p], modes_ref.at[p, me], sems, 0, o, span_to(o))
         out.start()
-        stage1.append((out, remote(inv_ref.at[p], modes_ref.at[p, s], sems, 0, o, span_to(o))))
+        stage1.append((out, remote(inv16.at[p], modes_ref.at[p, s], sems, 0, o, span_to(o))))
         stage2x.append((remote(modes_ref.at[p, s], modes_ref.at[p, s], sems, 1, o, xpeer),
                         remote(modes_ref.at[p, s], modes_ref.at[px, s], sems, 1, o, xpeer)))
         stage2c.append((remote(modes_ref.at[p, s], modes_ref.at[p, s], sems, 2, o, cpeer),
@@ -221,18 +246,27 @@
             parts.append(adj_ref[k // zdev, k % zdev, r:r + half, :])
         parts = swap_blocks(parts, share)
         for d in range(spans):
-            snd[d, i * half:(i + 1) * half, :] = parts[d]
+            stage[d, i * half:(i + 1) * half, :] = parts[d]
     parts = swap_blocks([tail[g] for g in range(spans)], share)
+    more = jnp.concatenate([a for a, _ in extra] + [b for _, b in extra], axis=0)
     for d in range(spans):
-        snd[d, sets * half:, :] = parts[d]
+        snd[d], scales = coded_blocks(stage[d], sets, half)
+        tsnd[d, :8] = jnp.concatenate([parts[d][:5]] + scales, axis=0)
+        tsnd[d, 8:] = more
+    tails = []
     fields, speeds = [], [[] for _ in range(NSTEP)]
     for o in range(1, spans):
         to, s = (me + o) % spans, (me + spans - o) % spans
         out = remote(snd.at[to], rcv.at[me], sems, 4, o, span_to(o))
         out.start()
         fields.append((out, remote(snd.at[to], rcv.at[s], sems, 4, o, span_to(o))))
+        out = remote(tsnd.at[to], trc.at[me], sems, 13, o, span_to(o))
+        out.start()
+        tails.append((out, remote(tsnd.at[to], trc.at[s], sems, 13, o, span_to(o))))
     own = pltpu.make_async_copy(snd.at[me], rcv.at[me], local_sem.at[0])
     own.start()
+    town = pltpu.make_async_copy(tsnd.at[me], trc.at[me], local_sem.at[2 + zdev])
+    town.start()
     wide = zdev * LANES
     for t in range(NSTEP):
         slot = step_ref[t]
@@ -247,7 +281,7 @@
             speeds[t].append((out, remote(vsnd.at[to, t], vrcv.at[s, t], sems, 5 + t, o, span_to(o))))
     vown = pltpu.make_async_copy(vsnd.at[me], vrcv.at[me], local_sem.at[1])
     vown.start()
-    mine = [pltpu.make_async_copy(inv_ref.at[j], modes_ref.at[j, me], local_sem.at[2 + j])
+    mine = [pltpu.make_async_copy(inv16.at[j], modes_ref.at[j, me], local_sem.at[2 + j])
             for j in range(zdev)]
     for c in mine:
         c.start()
@@ -273,15 +307,20 @@
         stage2x[o][1].wait_recv()
         stage3[o][0].start()
     own.wait()
-    for c in fields:
+    town.wait()
+    for c in fields + tails:
         c[1].wait_recv()
+    for s in range(spans):
+        x = rcv[s].astype(jnp.int32).astype(F32)
+        for i in range(sets):
+            stage[s, i * half:(i + 1) * half, :] = x[i * half:(i + 1) * half] * trc[s, 5 + i:6 + i, :]
     for i in range(sets):
-        parts = swap_blocks([rcv[s, i * half:(i + 1) * half, :] for s in range(spans)], share)
+        parts = swap_blocks([stage[s, i * half:(i + 1) * half, :] for s in range(spans)], share)
         for g in range(spans):
             h = spans * i + g
             k, r = h // 2, (h % 2) * half
             xs_ref[r:r + half, k * LANES:(k + 1) * LANES] = parts[g]
-    parts = swap_blocks([rcv[s, sets * half:, :] for s in range(spans)], share)
+    parts = swap_blocks([trc[s, :8, :] for s in range(spans)], share)
     for k in range(slabs):
         xs_ref[bulk:q, k * LANES:(k + 1) * LANES] = parts[k % spans][k // spans:k // spans + 1]
     for t in range(NSTEP):
@@ -313,7 +352,9 @@
                     c[1].wait_recv()
             for j in range(zdev):
                 for s in range(spans):
-                    high, low = split(modes_ref[j, s])
+                    x = decoded(modes_ref[j, s], trc[s, 8 + j:9 + j, :])
+                    x = jnp.where(eye, trc[s, 8 + zdev + j:9 + zdev + j, :], x)
+                    high, low = split(x)
                     modes_hi[j, s * qp:(s + 1) * qp, :] = high
                     modes_lo[j, s * qp:(s + 1) * qp, :] = low
         for j in range(zdev):
@@ -374,16 +415,20 @@
             parts.append(xs_ref[r:r + half, k * LANES:(k + 1) * LANES])
         parts = swap_blocks(parts, share)
         for d in range(spans):
-            bsnd[d, i * half:(i + 1) * half, :] = parts[d]
+            stage[d, i * half:(i + 1) * half, :] = parts[d]
     parts = swap_blocks([tail[g] for g in range(spans)], share)
     for d in range(spans):
-        bsnd[d, sets * half:, :] = parts[d]
+        bsnd[d], scales = coded_blocks(stage[d], sets, half)
+        tbsnd[d] = jnp.concatenate([parts[d][:5]] + scales, axis=0)
     rown.wait()
     for c in rows:
         c[1].wait_recv()
     part[...] = sum(rows_in[s] for s in range(planes))
     walls = exchange(9, spans, "span", lambda to: part.at[to], wrcv)
     returned = exchange(10, spans, "span", lambda to: bsnd.at[to], back)
+    returned += exchange(14, spans, "span", lambda to: tbsnd.at[to], tback)
+    tbown = pltpu.make_async_copy(tbsnd.at[me], tback.at[me], local_sem.at[2])
+    tbown.start()
     bown = pltpu.make_async_copy(bsnd.at[me], back.at[me], local_sem.at[1])
     bown.start()
     wown = pltpu.make_async_copy(part.at[me], wrcv.at[me], local_sem.at[0])
@@ -408,9 +453,10 @@
     for c in totals:
         c[1].wait_recv()
     bown.wait()
+    tbown.wait()
     for c in returned:
         c[1].wait_recv()
-    for group in (stage1, stage2x, stage2c, stage3, fields, *speeds, rows, walls, returned, squares, totals):
+    for group in (stage1, stage2x, stage2c, stage3, fields, tails, *speeds, rows, walls, returned, squares, totals):
         for c in group:
             c[0].wait_send()
 
@@ -426,7 +472,7 @@
     return one(a[0], b[0]) + (one(a[0], b[1]) + one(a[1], b[0]))
 
 
-def finish_kernel(spans, planes, zdev, q, count, back, weighted_ref, trcv, out_ref, grad_ref):
+def finish_kernel(spans, planes, zdev, q, count, back, tback, weighted_ref, trcv, out_ref, grad_ref, stage):
     share = LANES // spans
     bulk = q - 1
     half = bulk // 2
@@ -434,13 +480,17 @@
     sets = 2 * slabs // spans
     full = jnp.sum(sum(trcv[s] for s in range(planes))[0:1], axis=1, keepdims=True)
     grad_ref[...] = weighted_ref[...] * lax.rsqrt(full / count + 1e-06)
+    for s in range(spans):
+        x = back[s].astype(jnp.int32).astype(F32)
+        for i in range(sets):
+            stage[s, i * half:(i + 1) * half, :] = x[i * half:(i + 1) * half] * tback[s, 5 + i:6 + i, :]
     for i in range(sets):
-        parts = swap_blocks([back[s, i * half:(i + 1) * half, :] for s in range(spans)], share)
+        parts = swap_blocks([stage[s, i * half:(i + 1) * half, :] for s in range(spans)], share)
         for g in range(spans):
             h = spans * i + g
             k, r = h // 2, (h % 2) * half
             out_ref[k // zdev, r:r + half, k % zdev, :] = parts[g]
-    parts = swap_blocks([back[s, sets * half:, :] for s in range(spans)], share)
+    parts = swap_blocks([tback[s] for s in range(spans)], share)
     for k in range(slabs):
         out_ref[k // zdev, bulk:q, k % zdev, :] = parts[k % spans][k // spans:k // spans + 1]
 
@@ -480,23 +530,29 @@
     wall_count = wall_element.shape[0]
     qp = -(-q // 16) * 16
     bulk, wide = q - 1, zdev * LANES
-    rows = 3 * zdev * bulk // spans + 8
-    inverse = jnp.pad(helmholtz_inverse, ((0, 0), (0, qp - q), (0, LANES - q)))
+    rows = 3 * zdev * bulk // spans
+    inverse = helmholtz_inverse.transpose(1, 0, 2)
     shape = jax.ShapeDtypeStruct
     basis, diff, place = tables(spans, zdev, q, qp)
-    back, weighted, squares = pl.pallas_call(
+    back, tback, weighted, squares = pl.pallas_call(
         functools.partial(step_kernel, spans, planes, zdev, q, qp),
-        out_shape=(shape((spans, rows, LANES), F32), shape((zdev, wall_count // planes), F32),
+        out_shape=(shape((spans, rows, LANES), jnp.int16), shape((spans, 8, LANES), F32),
+                   shape((zdev, wall_count // planes), F32),
                    shape((planes, 8, LANES), F32)),
         in_specs=[pl.BlockSpec(memory_space=pltpu.SMEM)] + vmem(10),
-        out_specs=tuple(vmem(3)),
+        out_specs=tuple(vmem(4)),
         scratch_shapes=[
             pltpu.VMEM((qp, 3 * wide), F32),
             pltpu.VMEM((NSTEP, 2, qp, wide), F32),
-            pltpu.VMEM((zdev, spans, qp, LANES), F32),
+            pltpu.VMEM((qp, LANES), F32),
+            pltpu.VMEM((zdev, qp, LANES), jnp.int16),
+            pltpu.VMEM((zdev, spans, qp, LANES), jnp.int16),
             pltpu.VMEM((spans, 8, LANES), F32),
             pltpu.VMEM((spans, rows, LANES), F32),
-            pltpu.VMEM((spans, rows, LANES), F32),
+            pltpu.VMEM((spans, rows, LANES), jnp.int16),
+            pltpu.VMEM((spans, 8 + 2 * zdev, LANES), F32),
+            pltpu.VMEM((spans, rows, LANES), jnp.int16),
+            pltpu.VMEM((spans, 8 + 2 * zdev, LANES), F32),
             pltpu.VMEM((spans, NSTEP, bulk, LANES), BF16),
             pltpu.VMEM((spans, NSTEP, bulk, LANES), BF16),
             pltpu.VMEM((3 * qp, wide), F32),
@@ -504,7 +560,8 @@
             pltpu.VMEM((qp, wide), F32),
             pltpu.VMEM((zdev, spans * qp, LANES), BF16),
             pltpu.VMEM((zdev, spans * qp, LANES), BF16),
-            pltpu.VMEM((spans, rows, LANES), F32),
+            pltpu.VMEM((spans, rows, LANES), jnp.int16),
+            pltpu.VMEM((spans, 8, LANES), F32),
             pltpu.VMEM((planes, spans, 8, LANES), F32),
             pltpu.VMEM((planes, spans, 8, LANES), F32),
             pltpu.VMEM((spans, 8, LANES), F32),
@@ -512,8 +569,8 @@
             pltpu.VMEM((8, LANES), F32),
             pltpu.VMEM((spans, 8, LANES), F32),
             pltpu.VMEM((8, LANES), F32),
-            pltpu.SemaphoreType.DMA((2, 13, spans)),
-            pltpu.SemaphoreType.DMA((2 + zdev,)),
+            pltpu.SemaphoreType.DMA((2, 15, spans)),
+            pltpu.SemaphoreType.DMA((3 + zdev,)),
         ],
         compiler_params=pltpu.CompilerParams(collective_id=0, has_side_effects=True),
         name="steps",
@@ -522,10 +579,11 @@
     field, gradient = pl.pallas_call(
         functools.partial(finish_kernel, spans, planes, zdev, q, float(spans * zdev * wall_count)),
         out_shape=(shape((3, q, zdev, LANES), F32), shape((zdev, wall_count // planes), F32)),
-        in_specs=vmem(3),
+        in_specs=vmem(4),
         out_specs=tuple(vmem(2)),
+        scratch_shapes=[pltpu.VMEM((spans, rows, LANES), F32)],
         name="finish",
-    )(back, weighted, squares)
+    )(back, tback, weighted, squares)
     return field.transpose(0, 2, 1, 3), gradient
 
 

time: 84.6 us -> 70.7 us (0.84)
  Pallas kernels: 78.8 us -> 65.2 us
    pallas_call x1, Pallas kernels: 76.1 us -> 62.6 us  [kernels_on_device(): pl.pallas_call(functools.partial(step_kernel, spans, planes, zdev, q, qp)...]
    unnamed x5 -> x2, local copies, waits for them, and re-layouts: 4.31 us -> 4.56 us
where the time goes in v4:
time: 70.7 us; the launch traced here: 70.4 us
  Pallas kernels  65.2 us (92%)
  local copies, waits for them, and re-layouts  4.56 us (6%)
    pallas_call x1, Pallas kernels, kernels_on_device(): pl.pallas_call(functools.partial(step_kernel, spans, planes, zdev, q, qp)...  62.6 us
    unnamed x2, local copies, waits for them, and re-layouts  4.56 us
    pallas_call x1, Pallas kernels, kernels_on_device(): pl.pallas_call(functools.partial(finish_kernel, spans, planes, zdev, q, f...  2.58 us

profile of v4, /device:TPU:0, one launch (start us, length us, event | category | flops | bytes accessed | tf_op | source)
XLA Modules:
  0.0 70.4 jit_solution(10405648282126695484)
XLA Ops:
  0.6 1.9 %copy.13.adj_ref = f32[3,4,81,128]{3,2,1,0:T(8,128)} copy(f32[3,4,81,128]{3,1,2,0:T(4,128)} %param.11) | data formatting | bytes 995328 | tf_op args[0]
  2.5 2.7 %copy.14.ck_ref = bf16[8,2,4,81,128]{4,3,2,1,0:T(8,128)(2,1)} copy(bf16[8,2,4,81,128]{4,2,3,1,0:T(4,128)(2,1)} %param.12) | data formatting | bytes 2654208 | tf_op args[1]
  5.2 62.6 %steps.1 = (s16[8,120,128]{2,1,0:T(8,128)(2,1)}, f32[8,8,128]{2,1,0:T(8,128)}, f32[4,256]{1,0:T(4,128)}, f32[4,8,128]{2,1,0:T(8,128)}) custom-call(s32[3]{0:T(128)} %step_ref.1, f32[3,4,81,128]{3,2,1,0:T(8,128)} %copy.13.adj_ref, bf16[8,2,4,81,128]{4,3,2,1,0:T(8,128)(2,1)} %copy.14.ck_ref, f32[81,4,81]{2,1,0:T(4,128)} %bitcast.4, f32[2,128]{1,0:T(2,128)} %metric_ref.1, ...), custom_call_target="tpu_custom_call" | custom-call | tf_op jit(solution)/shard_map/steps/pallas_call | solution.py:537
  67.8 2.6 %finish.1 = (f32[3,81,4,128]{3,2,1,0:T(4,128)}, f32[4,256]{1,0:T(4,128)}) custom-call(s16[8,120,128]{2,1,0:T(8,128)(2,1)} %get-tuple-element.8.back, f32[8,8,128]{2,1,0:T(8,128)} %get-tuple-element.9.tback, f32[4,256]{1,0:T(4,128)} %get-tuple-element.10.weighted_ref, f32[4,8,128]{2,1,0:T(8,128)} %get-tuple-element.11.trcv), custom_call_target="tpu_custom_call" | custom-call | tf_op jit(solution)/shard_map/finish/pallas_call | solution.py:579

commit v5 on v4

--- a/solution.py
+++ b/solution.py
@@ -189,7 +189,7 @@
                 basis_ref, diff_ref, place_ref,
                 back, tback, weighted_ref, trcv,
                 xs_ref, vs_ref, padded, inv16, modes_ref, tail, stage, snd, tsnd, rcv, trc, vsnd, vrcv,
-                coef, solved, product, modes_hi, modes_lo, bsnd, tbsnd,
+                coef, solved, product, modes_cat, bsnd, tbsnd,
                 wall, rows_in, part, wrcv, square, srcv, total, sems, local_sem):
     share = LANES // spans
     me, p = lax.axis_index("span"), lax.axis_index("plane")
@@ -296,6 +296,7 @@
         scale = scale + pltpu.roll(scale, k, 1)
         k *= 2
     block = lax.broadcasted_iota(jnp.int32, (1, 3 * LANES), 1) % LANES // share
+    gap = jnp.zeros((LANES - qp, 3 * LANES), BF16)
     first = jnp.concatenate([scale[0:1]] * zdev, axis=1)
     second = jnp.concatenate([scale[1:2]] * zdev, axis=1)
 
@@ -340,9 +341,10 @@
         v1 = vs_ref[t, 1] * second
         for c in range(3):
             x = xs_ref[:, c * wide:(c + 1) * wide]
-            d = mul3((diff_ref[0], diff_ref[1]), split(x))
+            high, low = split(x)
+            d = dot(diff_ref[...], jnp.concatenate([high, low, high], axis=0))
             coef[c * qp:(c + 1) * qp, :] = x + v0 * d[:qp] + v1 * d[qp:]
-        y = mul3(split(coef[...]), (basis_ref[0], basis_ref[1]))
+        y = transform(coef[...], basis_ref, False)
         coef[...] = y
         if t == 0:
             for c in mine:
@@ -355,18 +357,20 @@
                     x = decoded(modes_ref[j, s], trc[s, 8 + j:9 + j, :])
                     x = jnp.where(eye, trc[s, 8 + zdev + j:9 + zdev + j, :], x)
                     high, low = split(x)
-                    modes_hi[j, s * qp:(s + 1) * qp, :] = high
-                    modes_lo[j, s * qp:(s + 1) * qp, :] = low
+                    modes_cat[j, s * qp:(s + 1) * qp, :LANES] = high
+                    modes_cat[j, s * qp:(s + 1) * qp, LANES:2 * LANES] = high
+                    modes_cat[j, s * qp:(s + 1) * qp, 2 * LANES:] = low
         for j in range(zdev):
             lanes = slice(j * LANES, (j + 1) * LANES)
             x = jnp.concatenate([coef[c * qp:(c + 1) * qp, lanes] for c in range(3)], axis=1)
-            r = mul3((modes_hi[j, :, :qp], modes_lo[j, :, :qp]), split(x))
+            high, low = split(x)
+            r = dot(modes_cat[j], jnp.concatenate([high, gap, low, gap, high, gap], axis=0))
             acc = r[:qp]
             for s in range(1, spans):
                 acc = jnp.where(block == s, r[s * qp:(s + 1) * qp], acc)
             for c in range(3):
                 solved[c * qp:(c + 1) * qp, lanes] = acc[:, c * LANES:(c + 1) * LANES]
-        y = mul3(split(solved[...]), (basis_ref[0], basis_ref[1]), ((1,), (1,)))
+        y = transform(solved[...], basis_ref, True)
         for c in range(3):
             xs_ref[:, c * wide:(c + 1) * wide] = y[c * qp:(c + 1) * qp]
         product[...] += y[qp:2 * qp] * vs_ref[t, 1]
@@ -380,30 +384,6 @@
             out.start()
             pairs.append((out, remote(pick_src(to), dst.at[s], sems, kind, o, {axis: to})))
         return pairs
-
-    high, low = split(product[...].T)
-    base = p * LANES + me * share
-    mode = lax.broadcasted_iota(jnp.int32, (qp, LANES), 0)
-    near = lax.broadcasted_iota(jnp.int32, (LANES, LANES), 0) % share + base
-    for piece in range(planes):
-        acc = 0.0
-        for h in range(2):
-            lo = (piece * 2 + h) * LANES
-            got = 0.0
-            for k in range(2):
-                pick = jnp.where(local_ref[k:k + 1, lo:lo + LANES] == mode, 1.0, 0.0).astype(BF16)
-                keep = jnp.where(elem_ref[k:k + 1, lo:lo + LANES] == near, 1.0, 0.0)
-                keep = jnp.concatenate([keep] * zdev, axis=0)
-                one = jnp.dot(high, pick, preferred_element_type=F32)
-                one = one + jnp.dot(low, pick, preferred_element_type=F32)
-                got = got + one * keep
-            for v in split(got):
-                acc = acc + jnp.dot(place_ref[h], v, preferred_element_type=F32)
-        for s in range(spans):
-            wall[piece, s] = acc[s * 8:(s + 1) * 8]
-    rows = exchange(8, planes, "plane", lambda to: wall.at[to], rows_in)
-    rown = pltpu.make_async_copy(wall.at[p], rows_in.at[p], local_sem.at[0])
-    rown.start()
 
     for k in range(slabs):
         tail[k % spans, k // spans:k // spans + 1, :] = xs_ref[bulk:q, k * LANES:(k + 1) * LANES]
@@ -420,17 +400,39 @@
     for d in range(spans):
         bsnd[d], scales = coded_blocks(stage[d], sets, half)
         tbsnd[d] = jnp.concatenate([parts[d][:5]] + scales, axis=0)
-    rown.wait()
-    for c in rows:
-        c[1].wait_recv()
-    part[...] = sum(rows_in[s] for s in range(planes))
-    walls = exchange(9, spans, "span", lambda to: part.at[to], wrcv)
     returned = exchange(10, spans, "span", lambda to: bsnd.at[to], back)
     returned += exchange(14, spans, "span", lambda to: tbsnd.at[to], tback)
     tbown = pltpu.make_async_copy(tbsnd.at[me], tback.at[me], local_sem.at[2])
     tbown.start()
     bown = pltpu.make_async_copy(bsnd.at[me], back.at[me], local_sem.at[1])
     bown.start()
+    high, low = split(product[...].T)
+    left = jnp.concatenate([high, low], axis=1)
+    pair = 2 * LANES
+    base = p * LANES + me * share
+    mode = lax.broadcasted_iota(jnp.int32, (qp, pair), 0)
+    near = lax.broadcasted_iota(jnp.int32, (LANES, pair), 0) % share + base
+    for piece in range(planes):
+        lanes = slice(piece * pair, (piece + 1) * pair)
+        got = 0.0
+        for k in range(2):
+            pick = jnp.where(local_ref[k:k + 1, lanes] == mode, 1.0, 0.0).astype(BF16)
+            keep = jnp.where(elem_ref[k:k + 1, lanes] == near, 1.0, 0.0)
+            keep = jnp.concatenate([keep] * zdev, axis=0)
+            got = got + dot(left, jnp.concatenate([pick, pick], axis=0)) * keep
+        acc = dot(place_ref[...], jnp.concatenate(split(got), axis=0))
+        acc = acc[:, :LANES] + pltpu.roll(acc[:, LANES:], zdev, 0)
+        for s in range(spans):
+            wall[piece, s] = acc[s * 8:(s + 1) * 8]
+    rows = exchange(8, planes, "plane", lambda to: wall.at[to], rows_in)
+    rown = pltpu.make_async_copy(wall.at[p], rows_in.at[p], local_sem.at[0])
+    rown.start()
+
+    rown.wait()
+    for c in rows:
+        c[1].wait_recv()
+    part[...] = sum(rows_in[s] for s in range(planes))
+    walls = exchange(9, spans, "span", lambda to: part.at[to], wrcv)
     wown = pltpu.make_async_copy(part.at[me], wrcv.at[me], local_sem.at[0])
     wown.start()
     wown.wait()
@@ -466,10 +468,16 @@
     return high, (x - high.astype(F32)).astype(BF16)
 
 
-def mul3(a, b, dims=((1,), (0,))):
-    def one(x, y):
-        return lax.dot_general(x, y, (dims, ((), ())), preferred_element_type=F32)
-    return one(a[0], b[0]) + (one(a[0], b[1]) + one(a[1], b[0]))
+def dot(a, b, dims=((1,), (0,))):
+    return lax.dot_general(a, b, (dims, ((), ())), preferred_element_type=F32)
+
+
+def transform(x, basis_ref, back):
+    high, low = split(x)
+    left = jnp.concatenate([high, high, low], axis=1)
+    parts = [basis_ref[0], basis_ref[1], basis_ref[0]]
+    right = jnp.concatenate(parts, axis=1 if back else 0)
+    return dot(left, right, ((1,), (1,)) if back else ((1,), (0,)))
 
 
 def finish_kernel(spans, planes, zdev, q, count, back, tback, weighted_ref, trcv, out_ref, grad_ref, stage):
@@ -511,13 +519,15 @@
     diff = np.zeros((2 * qp, qp))
     diff[:q, :q] = np.kron(matrix, np.eye(side))
     diff[qp:qp + q, :q] = np.kron(np.eye(side), matrix)
-    place = np.zeros((2, spans * 8, zdev * LANES), ml_dtypes.bfloat16)
-    for h in range(2):
-        for s in range(spans):
-            for z in range(zdev):
-                at = z * LANES + s * share
-                place[h, s * 8 + h * zdev + z, at:at + share] = 1.0
-    return halves(basis), halves(diff), place
+    place = np.zeros((spans * 8, zdev * LANES), ml_dtypes.bfloat16)
+    for s in range(spans):
+        for z in range(zdev):
+            at = z * LANES + s * share
+            place[s * 8 + z, at:at + share] = 1.0
+    high, low = halves(diff)
+    diff = np.concatenate([high, high, low], axis=1)
+    place = np.concatenate([place, place], axis=1)
+    return halves(basis), diff, place
 
 
 def vmem(n):
@@ -558,8 +568,7 @@
             pltpu.VMEM((3 * qp, wide), F32),
             pltpu.VMEM((3 * qp, wide), F32),
             pltpu.VMEM((qp, wide), F32),
-            pltpu.VMEM((zdev, spans * qp, LANES), BF16),
-            pltpu.VMEM((zdev, spans * qp, LANES), BF16),
+            pltpu.VMEM((zdev, spans * qp, 3 * LANES), BF16),
             pltpu.VMEM((spans, rows, LANES), jnp.int16),
             pltpu.VMEM((spans, 8, LANES), F32),
             pltpu.VMEM((planes, spans, 8, LANES), F32),

time: 70.7 us -> 64.1 us (0.907)
  Pallas kernels: 65.2 us -> 58.7 us
    pallas_call x1, Pallas kernels: 62.6 us -> 56.1 us  [kernels_on_device(): pl.pallas_call(functools.partial(step_kernel, spans, planes, zdev, q, qp)...]
where the time goes in v5:
time: 64.1 us; the launch traced here: 63.9 us
  Pallas kernels  58.7 us (92%)
  local copies, waits for them, and re-layouts  4.56 us (7%)
    pallas_call x1, Pallas kernels, kernels_on_device(): pl.pallas_call(functools.partial(step_kernel, spans, planes, zdev, q, qp)...  56.1 us
    unnamed x2, local copies, waits for them, and re-layouts  4.56 us
    pallas_call x1, Pallas kernels, kernels_on_device(): pl.pallas_call(functools.partial(finish_kernel, spans, planes, zdev, q, f...  2.58 us

profile of v5, /device:TPU:0, one launch (start us, length us, event | category | flops | bytes accessed | tf_op | source)
XLA Modules:
  0.0 63.9 jit_solution(4179950597995847540)
XLA Ops:
  0.6 1.9 %copy.13.adj_ref = f32[3,4,81,128]{3,2,1,0:T(8,128)} copy(f32[3,4,81,128]{3,1,2,0:T(4,128)} %param.11) | data formatting | bytes 995328 | tf_op args[0]
  2.5 2.7 %copy.14.ck_ref = bf16[8,2,4,81,128]{4,3,2,1,0:T(8,128)(2,1)} copy(bf16[8,2,4,81,128]{4,2,3,1,0:T(4,128)(2,1)} %param.12) | data formatting | bytes 2654208 | tf_op args[1]
  5.2 56.1 %steps.1 = (s16[8,120,128]{2,1,0:T(8,128)(2,1)}, f32[8,8,128]{2,1,0:T(8,128)}, f32[4,256]{1,0:T(4,128)}, f32[4,8,128]{2,1,0:T(8,128)}) custom-call(s32[3]{0:T(128)} %step_ref.1, f32[3,4,81,128]{3,2,1,0:T(8,128)} %copy.13.adj_ref, bf16[8,2,4,81,128]{4,3,2,1,0:T(8,128)(2,1)} %copy.14.ck_ref, f32[81,4,81]{2,1,0:T(4,128)} %bitcast.4, f32[2,128]{1,0:T(2,128)} %metric_ref.1, ...), custom_call_target="tpu_custom_call" | custom-call | tf_op jit(solution)/shard_map/steps/pallas_call | solution.py:547
  61.3 2.6 %finish.1 = (f32[3,81,4,128]{3,2,1,0:T(4,128)}, f32[4,256]{1,0:T(4,128)}) custom-call(s16[8,120,128]{2,1,0:T(8,128)(2,1)} %get-tuple-element.8.back, f32[8,8,128]{2,1,0:T(8,128)} %get-tuple-element.9.tback, f32[4,256]{1,0:T(4,128)} %get-tuple-element.10.weighted_ref, f32[4,8,128]{2,1,0:T(8,128)} %get-tuple-element.11.trcv), custom_call_target="tpu_custom_call" | custom-call | tf_op jit(solution)/shard_map/finish/pallas_call | solution.py:588
